TPU v7x, 256 devices: a whole 4x4x8 slice. The times are simulated.
256 devices in a mesh: mesh: 8 (over z), rve: 32 (over y, x, core).
Axes of the slice: x: 4, y: 4, z: 8, core: 2. Of those that a mesh axis runs over, the one named last changes fastest.
Arguments:
- displacement: float32 [3, 1024], P(None, ('mesh', 'rve')), may hold values from -6 to 6
- shape_grads: float32 [3, 8, 4096], P(None, None, ('mesh', 'rve')), may hold values from -2 to 2
- point_weights: float32 [4096], P(('mesh', 'rve')), may hold values from 0.5 to 2
- conn: int32 [8, 512], P(None, ('mesh', 'rve')), may hold values from 0 to 143
- halo_nodes: int32 [2, 64], P(None, 'mesh'), may hold values from 0 to 127
- warm_strain: float32 [4096, 6, 4096], P(('mesh', 'rve')), may hold values from -4 to 4
- moduli: float32 [4096, 2, 4096], P(('mesh', 'rve')), may hold values from 0.2 to 2
- owner: int32 [4096], P(('mesh', 'rve')), may hold values from 0 to 31, as said below
- sweeps: int32 [4096], P(('mesh', 'rve')), may hold values from 1 to 2, as said below
Outputs:
- nodal_force: float32 [3, 1024], P(None, ('mesh', 'rve'))
- gp_stress: float32 [6, 4096], P(None, ('mesh', 'rve'))
- micro_strain: float32 [4096, 6, 4096], P(('mesh', 'rve'))
Inputs may be any that keep to these rules, and one draw needn't show every extreme that they name: The owner lies in the Gauss point's own mesh row. The 16 Gauss points of one device go 2 each to 8 different owners, and every owner receives exactly 16 Gauss points. `sweeps`: counts may be skewed by owner: all Gauss points of some owners take 2.
All inputs are finite; a program needn't handle non-finite values.
Results may differ from a plain program's by a relative error of at most 0.0003.
Values sent between devices are 32-bit elements; how exact they have to be, the bound alone decides.
A program may use at most 128 MiB of HBM per device.

v0:
```python
import math

import jax
import jax.numpy as jnp
from jax import lax
from jax.sharding import PartitionSpec as P

RES = 16


ref_modulus = 1.1
half_inverse = 1.0 / 2.2
coupling = 2.2 / (1.1 * 3.3)
index_pairs = ((0, 0), (1, 1), (2, 2), (1, 2), (0, 2), (0, 1))
diagonal_entries = (1.0, 1.0, 1.0, 0.0, 0.0, 0.0)


def from_everyone(shard, axis):
    size = lax.axis_size(axis)
    return lax.all_to_all(
        jnp.broadcast_to(shard[None], (size, *shard.shape)), axis, 0, 0, tiled=True
    )


def joined_along(tiles, dim):
    lengths = list(tiles.shape[1:])
    lengths[dim] *= tiles.shape[0]
    return jnp.moveaxis(tiles, 0, dim).reshape(lengths)


def collect(shard, axis, dim):
    tiles = from_everyone(shard, axis)
    return joined_along(tiles, dim)


def extended_2(shard, sides, width):
    for axis, dim in sides:
        size, length = (lax.axis_size(axis), shard.shape[dim])
        up = [(i, (i + 1) % size) for i in range(size - 1)]
        down = [(j, i) for i, j in up]
        last = lax.slice_in_dim(shard, length - width, length, axis=dim)
        first = lax.slice_in_dim(shard, 0, width, axis=dim)
        before = lax.ppermute(last, axis, up)
        after = lax.ppermute(first, axis, down)
        shard = jnp.concatenate([before, shard, after], axis=dim)
    return shard


def cut_along(shard, dim, size):
    lengths = shard.shape
    tiles = shard.reshape(*lengths[:dim], size, lengths[dim] // size, *lengths[dim + 1 :])
    return jnp.moveaxis(tiles, dim, 0)


def sum_at_owner(shard, axis, dim):
    tiles = cut_along(shard, dim, lax.axis_size(axis))
    arrived = lax.all_to_all(tiles, axis, split_axis=0, concat_axis=0, tiled=True)
    return arrived.sum(axis=0)


def unit_normals(grid_side):
    wave = jnp.arange(grid_side, dtype=jnp.int32)
    signed = jnp.where(wave < grid_side // 2, wave, wave - grid_side).astype(jnp.float32)
    cube = (grid_side, grid_side, grid_side)
    along_x = jnp.broadcast_to(signed[:, None, None], cube).reshape(-1)
    along_y = jnp.broadcast_to(signed[None, :, None], cube).reshape(-1)
    along_z = jnp.broadcast_to(signed[None, None, :], cube).reshape(-1)
    length_sq = along_x * along_x + along_y * along_y + along_z * along_z
    safe_length = jnp.sqrt(jnp.where(length_sq > 0, length_sq, 1.0))
    inverse_len = jnp.where(length_sq > 0, 1.0 / safe_length, 0.0)
    return jnp.stack([along_x * inverse_len, along_y * inverse_len, along_z * inverse_len])


def transform_tables(grid_side):
    wave = jnp.arange(grid_side, dtype=jnp.int32)
    phase = wave[:, None] * wave[None, :] % grid_side
    angle = phase.astype(jnp.float32) * (2.0 * math.pi / grid_side)
    plane_phase = (
        wave[:, None, None, None] * wave[None, None, :, None]
        + wave[None, :, None, None] * wave[None, None, None, :]
    ) % grid_side
    plane_angle = plane_phase.reshape(grid_side * grid_side, grid_side * grid_side).astype(
        jnp.float32
    ) * (2.0 * math.pi / grid_side)
    plane_cos = jnp.cos(plane_angle)
    plane_sin = jnp.sin(plane_angle)
    forward_plane = jnp.concatenate([plane_cos, -plane_sin], axis=1)
    inverse_plane = jnp.concatenate([plane_cos, -plane_sin], axis=0)
    return (jnp.cos(angle), jnp.sin(angle), forward_plane, inverse_plane)


def product(left, right):
    return jnp.dot(left, right, preferred_element_type=jnp.float32, precision=lax.Precision.HIGHEST)


def line_product(table, field):
    return jnp.einsum("ab,mbc->mac", table, field, precision=lax.Precision.HIGHEST)


def to_spectrum(polar, tables):
    line_cos, line_sin, forward_plane, inverse_plane = tables
    side = line_cos.shape[0]
    plane_size = side * side
    rows_total = polar.shape[0] * polar.shape[1]
    planed = product(polar.reshape(rows_total * side, plane_size), forward_plane).reshape(
        rows_total, side, 2 * plane_size
    )
    cos_part = line_product(line_cos, planed)
    sin_part = line_product(line_sin, planed)
    real_full = cos_part[..., :plane_size] + sin_part[..., plane_size:]
    imag_full = cos_part[..., plane_size:] - sin_part[..., :plane_size]
    return (real_full.reshape(polar.shape), imag_full.reshape(polar.shape))


def from_spectrum(real_part, imag_part, tables):
    line_cos, line_sin, forward_plane, inverse_plane = tables
    side = line_cos.shape[0]
    plane_size = side * side
    rows_total = real_part.shape[0] * real_part.shape[1]
    joined = jnp.concatenate(
        [
            real_part.reshape(rows_total, side, plane_size),
            imag_part.reshape(rows_total, side, plane_size),
        ],
        axis=2,
    )
    cos_part = line_product(line_cos, joined)
    sin_part = line_product(line_sin, joined)
    lined = jnp.concatenate(
        [
            cos_part[..., :plane_size] - sin_part[..., plane_size:],
            cos_part[..., plane_size:] + sin_part[..., :plane_size],
        ],
        axis=2,
    )
    spatial = product(lined.reshape(rows_total * side, 2 * plane_size), inverse_plane)
    return spatial.reshape(real_part.shape) / float(side**3)


def green_apply(polar, normals):
    vectors = (normals[0], normals[1], normals[2])
    entries = [polar[..., component, :] for component in range(6)]
    traction_x = entries[0] * vectors[0] + entries[5] * vectors[1] + entries[4] * vectors[2]
    traction_y = entries[5] * vectors[0] + entries[1] * vectors[1] + entries[3] * vectors[2]
    traction_z = entries[4] * vectors[0] + entries[3] * vectors[1] + entries[2] * vectors[2]
    tractions = (traction_x, traction_y, traction_z)
    normal_load = vectors[0] * traction_x + vectors[1] * traction_y + vectors[2] * traction_z
    result = []
    for first_axis, second_axis in index_pairs:
        pair_term = (
            vectors[first_axis] * tractions[second_axis]
            + vectors[second_axis] * tractions[first_axis]
        )
        result.append(
            pair_term * half_inverse
            - coupling * vectors[first_axis] * vectors[second_axis] * normal_load
        )
    return jnp.stack(result, axis=-2)


def stress_of(strain_field, lame_first, shear_modulus):
    trace_sum = strain_field[:, 0] + strain_field[:, 1] + strain_field[:, 2]
    diagonal_mask = jnp.array(diagonal_entries, jnp.float32)
    return (
        2.0 * shear_modulus[:, None, :] * strain_field
        + (lame_first * trace_sum)[:, None, :] * diagonal_mask[None, :, None]
    )


def sweep_once(strain_field, macro_rows, lame_first, shear_modulus, normals, tables):
    trace_sum = strain_field[:, 0] + strain_field[:, 1] + strain_field[:, 2]
    diagonal_mask = jnp.array(diagonal_entries, jnp.float32)
    polar = 2.0 * (shear_modulus - ref_modulus)[:, None, :] * strain_field
    polar = (
        polar + ((lame_first - ref_modulus) * trace_sum)[:, None, :] * diagonal_mask[None, :, None]
    )
    real_part, imag_part = to_spectrum(polar, tables)
    fluctuation = from_spectrum(
        green_apply(real_part, normals), green_apply(imag_part, normals), tables
    )
    return macro_rows[:, :, None] - fluctuation


def make_advance(
    sweep_index, macro_rows, lame_first, shear_modulus, count_rows, normals, tables, strain_field
):
    updated = sweep_once(strain_field, macro_rows, lame_first, shear_modulus, normals, tables)
    return jnp.where((count_rows > sweep_index)[:, None, None], updated, strain_field)


def relax_points(start_field, macro_rows, moduli_rows, count_rows, normals, tables):
    lame_first = moduli_rows[:, 0]
    shear_modulus = moduli_rows[:, 1]
    strain_field = start_field
    for sweep_index in range(2):
        strain_field = make_advance(
            sweep_index,
            macro_rows,
            lame_first,
            shear_modulus,
            count_rows,
            normals,
            tables,
            strain_field,
        )
    mean_stress = jnp.mean(stress_of(strain_field, lame_first, shear_modulus), axis=2)
    return (strain_field, mean_stress)


def on_device(
    displacement, shape_grads, point_weights, conn, halo_nodes, warm_strain, moduli, owner, sweeps
):
    highest = lax.Precision.HIGHEST
    point_count = warm_strain.shape[0]
    voxel_count = warm_strain.shape[2]
    owner_span = lax.axis_size("rve")
    per_owner = max(2, point_count // owner_span)
    slot_count = owner_span * per_owner
    gathered = collect(displacement, "rve", 1)
    nodes_part = gathered.shape[1]
    halo_width = halo_nodes.shape[1]
    outgoing = jnp.concatenate([gathered[:, halo_nodes[0]], gathered[:, halo_nodes[1]]], axis=1)
    face_values = extended_2(outgoing, (("mesh", 1),), halo_width)
    extended = jnp.concatenate(
        [gathered, face_values[:, :halo_width], face_values[:, 3 * halo_width :]], axis=1
    )
    elements = conn.shape[1]
    elem_disp = extended[:, conn]
    gradients = shape_grads.reshape(3, 8, elements, 8)
    grad_disp = jnp.einsum("iae,jaeq->ijeq", elem_disp, gradients, precision=highest).reshape(
        3, 3, point_count
    )
    macro_strain = jnp.stack(
        [
            grad_disp[0, 0],
            grad_disp[1, 1],
            grad_disp[2, 2],
            (grad_disp[1, 2] + grad_disp[2, 1]) * 0.5,
            (grad_disp[0, 2] + grad_disp[2, 0]) * 0.5,
            (grad_disp[0, 1] + grad_disp[1, 0]) * 0.5,
        ],
        axis=1,
    )
    start_field = (
        warm_strain - jnp.mean(warm_strain, axis=2, keepdims=True) + macro_strain[:, :, None]
    )
    normals = unit_normals(RES)
    tables = transform_tables(RES)
    local_index = jnp.arange(point_count, dtype=jnp.int32)
    same_owner = owner[:, None] == owner[None, :]
    earlier = local_index[None, :] < local_index[:, None]
    slot_rank = jnp.sum((same_owner & earlier).astype(jnp.int32), axis=1)
    slot_index = owner * per_owner + slot_rank
    final_field, stress_rows = relax_points(
        start_field, macro_strain, moduli, sweeps, normals, tables
    )
    send_field = (
        jnp.zeros((slot_count, 6, voxel_count), jnp.float32).at[slot_index].set(final_field)
    )
    send_flag = jnp.zeros((slot_count,), jnp.float32).at[slot_index].set(1.0)
    received = (
        lax.all_to_all(send_field, "rve", split_axis=0, concat_axis=0, tiled=True),
        lax.all_to_all(send_flag, "rve", split_axis=0, concat_axis=0, tiled=True),
    )
    filled = jnp.nonzero(received[1] > 0.5, size=point_count)[0].astype(jnp.int32)
    micro_strain = received[0][filled]
    comps = stress_rows.T
    symmetric = jnp.stack(
        [
            jnp.stack([comps[0], comps[5], comps[4]]),
            jnp.stack([comps[5], comps[1], comps[3]]),
            jnp.stack([comps[4], comps[3], comps[2]]),
        ]
    )
    weighted = symmetric * point_weights[None, None, :]
    element_force = jnp.einsum(
        "ijeq,jaeq->iae", weighted.reshape(3, 3, elements, 8), gradients, precision=highest
    )
    spread = jnp.zeros((3, nodes_part + 2 * halo_width), jnp.float32).at[:, conn].add(element_force)
    outgoing_force = jnp.concatenate(
        [spread[:, nodes_part : nodes_part + halo_width], spread[:, nodes_part + halo_width :]],
        axis=1,
    )
    arrived = extended_2(outgoing_force, (("mesh", 1),), halo_width)
    own_part = spread[:, :nodes_part].at[:, halo_nodes[0]].add(arrived[:, :halo_width])
    own_part = own_part.at[:, halo_nodes[1]].add(arrived[:, 3 * halo_width :])
    nodal_force = sum_at_owner(own_part, "rve", 1)
    return (nodal_force, comps, micro_strain)


def solution(mesh):
    in_specs = (
        P(None, ("mesh", "rve")),
        P(None, None, ("mesh", "rve")),
        P(("mesh", "rve")),
        P(None, ("mesh", "rve")),
        P(None, "mesh"),
        P(("mesh", "rve"), None, None),
        P(("mesh", "rve"), None, None),
        P(("mesh", "rve")),
        P(("mesh", "rve")),
    )
    out_specs = (P(None, ("mesh", "rve")), P(None, ("mesh", "rve")), P(("mesh", "rve"), None, None))
    return jax.shard_map(
        on_device, mesh=mesh, in_specs=in_specs, out_specs=out_specs, check_vma=False
    )
```

profile of v0, /device:TPU:96, one launch (start us, length us, event | category | flops | bytes accessed | tf_op | source)
XLA Modules:
  0.0 330.3 jit_solution(9647622500769895474)
XLA Ops:
  2.1 7.3 %all-to-all-start = ((f32[32,3,4]{1,2,0:T(4,128)}), f32[32,3,4]{1,2,0:T(4,128)S(1)}, u32[]{:S(2)}, u32[]{:S(2)}) async-start(f32[32,3,4]{1,2,0:T(4,128)} %broadcast_in_dim.691), calls=%async_computation | async-start | bytes 131072 | tf_op jit(solution)/shard_map/all_to_all | solution.py:20
  21.0 7.4 %all-to-all-start.3 = ((f32[32,2,1]{1,2,0:T(1,128)}), f32[32,2,1]{1,2,0:T(1,128)S(1)}, u32[]{:S(2)}, u32[]{:S(2)}) async-start(f32[32,2,1]{1,2,0:T(1,128)} %bitcast.46), calls=%async_computation.3 | async-start | bytes 32768 | tf_op jit(solution)/shard_map/all_to_all | solution.py:263
  31.5 5.0 %collective-permute-start = (f32[3,8]{0,1:T(8,128)S(1)}, f32[3,8]{0,1:T(8,128)S(1)}, u32[]{:S(2)}, u32[]{:S(2)}) collective-permute-start(f32[3,8]{0,1:T(8,128)S(1)} %bitcast.124), channel_id=1, source_target_pairs={{0,32},{32,64},{64,96},{96,128},{128,160},{160,192},{192,224},{1,3... | collective-permute-start | bytes 296 | tf_op jit(solution)/shard_map/ppermute | solution.py:43
  42.3 3.5 %dot_general.47 = f32[96,16,256]{2,1,0:T(8,128)} reshape(f32[16,6,4096]{2,1,0:T(8,128)} %copy.123) | data formatting | bytes 3145728 | tf_op jit(solution)/shard_map/dot_general | solution.py:93
  45.7 4.2 %fusion.3 = f32[96,16,512]{2,1,0:T(8,128)S(1)} fusion(f32[96,16,256]{2,1,0:T(8,128)} %dot_general.47, f32[256,256]{1,0:T(8,128)S(1)} %get-tuple-element.78, f32[256,256]{1,0:T(8,128)S(1)} %get-tuple-element.77), kind=kOutput, calls=%fused_computation.44 | convolution fusion | flops 2416050176 | bytes 5242880 | tf_op jit(solution)/shard_map/dot_general | solution.py:93
  50.0 3.1 convolution_bitcast_fusion.6
  53.1 3.2 convolution_bitcast_fusion.7
  58.5 3.0 reshape.3112
  61.5 7.7 %fusion.141 = (f32[16,1,4096]{2,1,0:T(1,128)S(1)}, f32[16,1,4096]{2,1,0:T(1,128)S(1)}, f32[16,1,4096]{2,1,0:T(1,128)}, f32[16,1,4096]{2,1,0:T(1,128)}, f32[16,1,4096]{2,1,0:T(1,128)}, /*index=5*/f32[16,1,4096]{2,1,0:T(1,128)}) fusion(f32[16,6,4096]{2,1,0:T(8,128)} %reshape.3112), kind=kLoop, calls=%fused_computation.261 | loop fusion | bytes 3145728 | tf_op jit(solution)/shard_map/slice | solution.py:142
  72.1 7.1 %fusion.142 = (f32[16,1,4096]{2,1,0:T(1,128)S(1)}, f32[16,1,4096]{2,1,0:T(1,128)S(1)}, f32[16,1,4096]{2,1,0:T(1,128)S(1)}, f32[16,1,4096]{2,1,0:T(1,128)S(1)}, f...) fusion(f32[16,6,4096]{2,1,0:T(8,128)} %reshape.3110), kind=kLoop, calls=%fused_computation.262 | loop fusion | bytes 3145728 | tf_op jit(solution)/shard_map/slice | solution.py:142
  79.3 2.9 subtract_dynamic-update-slice_fusion.17
  86.6 3.0 reshape.3111
  89.6 2.9 constant_dynamic-update-slice_fusion.1
  94.8 3.2 reshape.3113
  100.7 5.2 %convolution_bitcast_fusion.4 = f32[96,16,512]{2,1,0:T(8,128)S(1)} fusion(f32[96,16,512]{2,1,0:T(8,128)} %constant_dynamic-update-slice_fusion), kind=kOutput, calls=%fused_computation.18 | convolution fusion | flops 150998528 | bytes 6291456 | tf_op jit(solution)/shard_map/ab,mbc->mac/dot_general | solution.py:97
  105.9 3.2 convolution_bitcast_fusion.5
  110.1 3.8 %convolution_multiply_fusion.1 = f32[1536,256]{1,0:T(8,128)} fusion(f32[1536,512]{1,0:T(8,128)S(1)} %bitcast.116, f32[256,256]{1,0:T(8,128)S(1)} %get-tuple-element.78, f32[256,256]{1,0:T(8,128)S(1)} %get-tuple-element.77), kind=kOutput, calls=%fused_computation.13 | convolution fusion | flops 2416443392 | bytes 5242880 | tf_op jit(solution)/shard_map/dot_general | solution.py:93
  113.9 3.2 div.34
  123.9 4.2 %fusion.2 = f32[96,16,512]{2,1,0:T(8,128)S(1)} fusion(f32[96,16,256]{2,1,0:T(8,128)} %dot_general.54, f32[256,256]{1,0:T(8,128)S(1)} %get-tuple-element.78, f32[256,256]{1,0:T(8,128)S(1)} %get-tuple-element.77), kind=kOutput, calls=%fused_computation.43 | convolution fusion | flops 2416050176 | bytes 5242880 | tf_op jit(solution)/shard_map/dot_general | solution.py:93
  128.1 3.1 convolution_bitcast_fusion.2
  131.3 3.3 %convolution_bitcast_fusion.3 = f32[96,16,512]{2,1,0:T(8,128)S(1)} fusion(f32[96,16,512]{2,1,0:T(8,128)S(1)} %fusion.2), kind=kOutput, calls=%fused_computation.17 | convolution fusion | flops 150998528 | bytes 6291456 | tf_op jit(solution)/shard_map/ab,mbc->mac/dot_general | solution.py:97
  144.2 2.9 subtract_dynamic-update-slice_fusion.5
  156.3 3.2 reshape.3118
  161.1 3.1 convolution_bitcast_fusion
  164.3 3.1 convolution_bitcast_fusion.1
  178.6 5.4 %collective-permute-start.2 = (f32[3,8]{0,1:T(8,128)S(1)}, f32[3,8]{0,1:T(8,128)S(1)}, u32[]{:S(2)}, u32[]{:S(2)}) collective-permute-start(f32[3,8]{0,1:T(8,128)S(1)} %get-tuple-element.80), channel_id=1, source_target_pairs={{0,32},{32,64},{64,96},{96,128},{128,160},{160,192},{192,224},{1,3... | collective-permute-start | bytes 296 | tf_op jit(solution)/shard_map/ppermute | solution.py:43
  192.8 7.4 %all-to-all-start.1 = ((f32[32,3,4]{1,2,0:T(4,128)}), f32[32,3,4]{1,2,0:T(4,128)S(1)}, u32[]{:S(2)}, u32[]{:S(2)}) async-start(f32[32,3,4]{1,2,0:T(4,128)} %bitcast.45), calls=%async_computation.1 | async-start | bytes 131072 | tf_op jit(solution)/shard_map/all_to_all | solution.py:57
  202.5 4.3 %broadcast_in_dim.696 = f32[64,6,4096]{2,1,0:T(8,128)} broadcast(f32[]{:T(128)} %constant.44.clone.1), dimensions={} | broadcast | bytes 6291460 | tf_op jit(solution)/shard_map/broadcast_in_dim | solution.py:258
  206.8 3.7 %scatter_fusion = f32[64,6,4096]{2,1,0:T(8,128)} fusion(f32[64,6,4096]{2,1,0:T(8,128)} %broadcast_in_dim.696, s32[16]{0:T(128)S(1)} %compare_select_fusion.5, f32[16,6,4096]{2,1,0:T(8,128)S(1)} %copy-done.4), kind=kCustom, calls=%fused_computation.7 | custom fusion | bytes 4718656 | tf_op jit(solution)/shard_map/scatter | solution.py:258
  210.5 7.5 %all-to-all-start.2 = ((f32[64,6,4096]{2,1,0:T(8,128)}), f32[64,6,4096]{2,1,0:T(8,128)}, u32[]{:S(2)}, u32[]{:S(2)}) async-start(f32[64,6,4096]{2,1,0:T(8,128)} %scatter_fusion), calls=%async_computation.2 | async-start | bytes 16777216 | tf_op jit(solution)/shard_map/all_to_all | solution.py:262
  221.6 102.3 %all-to-all-done.2 = f32[64,6,4096]{2,1,0:T(8,128)} async-done(((f32[64,6,4096]{2,1,0:T(8,128)}), f32[64,6,4096]{2,1,0:T(8,128)}, u32[]{:S(2)}, u32[]{:S(2)}) %all-to-all-start.2) | async-done | bytes 6291488 | tf_op jit(solution)/shard_map/all_to_all | solution.py:262
  323.9 4.1 %gather_fusion.3 = f32[16,6,4096]{2,1,0:T(8,128)S(1)} fusion(f32[64,6,4096]{2,1,0:T(8,128)} %all-to-all-done.2, s32[1024]{0:T(1024)S(1)} %pad_clamp_fusion), kind=kCustom, calls=%fused_computation.3 | custom fusion | bytes 3145792 | tf_op jit(solution)/shard_map/gather | solution.py:266
  (183 shorter events, 92.1 us)
Async XLA Ops:
  0.6 11.8 %copy-start.25 = (s32[2,8]{1,0:T(2,128)S(1)}, s32[2,8]{1,0:T(2,128)}, u32[]{:S(2)}) copy-start(s32[2,8]{1,0:T(2,128)} %param.16) | copy-start | bytes 196
  0.6 11.8 %copy-start.21 = (f32[16,2,4096]{2,1,0:T(2,128)S(1)}, f32[16,2,4096]{2,1,0:T(2,128)}, u32[]{:S(2)}) copy-start(f32[16,2,4096]{2,1,0:T(2,128)} %param.18) | copy-start | bytes 1572868
  2.1 18.9 %all-to-all-start = ((f32[32,3,4]{1,2,0:T(4,128)}), f32[32,3,4]{1,2,0:T(4,128)S(1)}, u32[]{:S(2)}, u32[]{:S(2)}) async-start(f32[32,3,4]{1,2,0:T(4,128)} %broadcast_in_dim.691), calls=%async_computation | async-start | bytes 131072 | tf_op jit(solution)/shard_map/all_to_all | solution.py:20
  13.0 106.8 %copy-start.7 = (f32[16,1,4096]{2,1,0:T(1,128)}, f32[16,1,4096]{2,1,0:T(1,128)S(1)}, u32[]{:S(2)}) copy-start(f32[16,1,4096]{2,1,0:T(1,128)S(1)} %get-tuple-element.74) | copy-start | bytes 786436
  15.5 3.7 %copy-start.26 = (s32[16]{0:T(128)S(1)}, s32[16]{0:T(128)}, u32[]{:S(2)}) copy-start(s32[16]{0:T(128)} %param.20) | copy-start | bytes 196
  15.5 3.7 %copy-start.27 = (s32[16]{0:T(128)S(1)}, s32[16]{0:T(128)}, u32[]{:S(2)}) copy-start(s32[16]{0:T(128)} %param.19) | copy-start | bytes 196
  15.5 4.0 %copy-start.23 = (f32[3,8,16]{2,1,0:T(8,128)S(1)}, f32[3,8,16]{2,1,0:T(8,128)}, u32[]{:S(2)}) copy-start(f32[3,8,16]{2,1,0:T(8,128)} %param.13) | copy-start | bytes 4612
  15.5 4.1 %copy-start.28 = (f32[16]{0:T(128)S(1)}, f32[16]{0:T(128)}, u32[]{:S(2)}) copy-start(f32[16]{0:T(128)} %param.14) | copy-start | bytes 196
  15.5 23.5 %copy-start = (f32[16,6,4096]{2,0,1:T(8,128)S(1)}, f32[16,6,4096]{2,0,1:T(8,128)}, u32[]{:S(2)}) copy-start(f32[16,6,4096]{2,0,1:T(8,128)} %param.17) | copy-start | bytes 4718596
  19.2 104.7 %copy-start.5 = (f32[256,256]{1,0:T(8,128)}, f32[256,256]{1,0:T(8,128)S(1)}, u32[]{:S(2)}) copy-start(f32[256,256]{1,0:T(8,128)S(1)} %get-tuple-element.78) | copy-start | bytes 786436
  21.0 171.8 %all-to-all-start.3 = ((f32[32,2,1]{1,2,0:T(1,128)}), f32[32,2,1]{1,2,0:T(1,128)S(1)}, u32[]{:S(2)}, u32[]{:S(2)}) async-start(f32[32,2,1]{1,2,0:T(1,128)} %bitcast.46), calls=%async_computation.3 | async-start | bytes 32768 | tf_op jit(solution)/shard_map/all_to_all | solution.py:263
  28.9 7.6 %collective-permute-start.1 = (f32[3,8]{0,1:T(8,128)S(1)}, f32[3,8]{0,1:T(8,128)S(1)}, u32[]{:S(2)}, u32[]{:S(2)}) collective-permute-start(f32[3,8]{0,1:T(8,128)S(1)} %bitcast.123), channel_id=1, source_target_pairs={{32,0},{64,32},{96,64},{128,96},{160,128},{192,160},{224,192},{33,... | collective-permute-start | bytes 296 | tf_op jit(solution)/shard_map/ppermute | solution.py:44
  31.5 6.4 %collective-permute-start = (f32[3,8]{0,1:T(8,128)S(1)}, f32[3,8]{0,1:T(8,128)S(1)}, u32[]{:S(2)}, u32[]{:S(2)}) collective-permute-start(f32[3,8]{0,1:T(8,128)S(1)} %bitcast.124), channel_id=1, source_target_pairs={{0,32},{32,64},{64,96},{96,128},{128,160},{160,192},{192,224},{1,3... | collective-permute-start | bytes 296 | tf_op jit(solution)/shard_map/ppermute | solution.py:43
  72.1 7.1 %copy-start.17 = (f32[16,1,4096]{2,1,0:T(1,128)S(1)}, f32[16,1,4096]{2,1,0:T(1,128)}, u32[]{:S(2)}) copy-start(f32[16,1,4096]{2,1,0:T(1,128)} %get-tuple-element.63) | copy-start | bytes 786436
  72.1 7.1 %copy-start.18 = (f32[16,1,4096]{2,1,0:T(1,128)S(1)}, f32[16,1,4096]{2,1,0:T(1,128)}, u32[]{:S(2)}) copy-start(f32[16,1,4096]{2,1,0:T(1,128)} %get-tuple-element.64) | copy-start | bytes 786436
  72.1 7.2 %copy-start.19 = (f32[16,1,4096]{2,1,0:T(1,128)S(1)}, f32[16,1,4096]{2,1,0:T(1,128)}, u32[]{:S(2)}) copy-start(f32[16,1,4096]{2,1,0:T(1,128)} %get-tuple-element.65) | copy-start | bytes 786436
  72.1 7.2 %copy-start.20 = (f32[16,1,4096]{2,1,0:T(1,128)S(1)}, f32[16,1,4096]{2,1,0:T(1,128)}, u32[]{:S(2)}) copy-start(f32[16,1,4096]{2,1,0:T(1,128)} %get-tuple-element.66) | copy-start | bytes 786436
  89.6 2.9 copy-start.12
  100.7 5.2 %copy-start.1 = (f32[96,16,512]{2,1,0:T(8,128)S(1)}, f32[96,16,512]{2,1,0:T(8,128)}, u32[]{:S(2)}) copy-start(f32[96,16,512]{2,1,0:T(8,128)} %constant_dynamic-update-slice_fusion) | copy-start | bytes 9437188
  142.6 1.5 copy-start.14
  142.6 1.5 copy-start.15
  142.6 1.5 copy-start.16
  152.2 1.9 copy-start.10
  171.6 1.8 copy-start.3
  173.5 2.7 copy-start.8
  173.5 2.9 copy-start.13
  176.8 25.7 %copy-start.22 = (f32[6,16]{1,0:T(8,128)}, f32[6,16]{1,0:T(8,128)S(1)}, u32[]{:S(2)}) copy-start(f32[6,16]{1,0:T(8,128)S(1)} %multiply_bitcast_fusion.2) | copy-start | bytes 1156
  178.6 7.3 %collective-permute-start.2 = (f32[3,8]{0,1:T(8,128)S(1)}, f32[3,8]{0,1:T(8,128)S(1)}, u32[]{:S(2)}, u32[]{:S(2)}) collective-permute-start(f32[3,8]{0,1:T(8,128)S(1)} %get-tuple-element.80), channel_id=1, source_target_pairs={{0,32},{32,64},{64,96},{96,128},{128,160},{160,192},{192,224},{1,3... | collective-permute-start | bytes 296 | tf_op jit(solution)/shard_map/ppermute | solution.py:43
  184.0 6.7 %collective-permute-start.3 = (f32[3,8]{0,1:T(8,128)S(1)}, f32[3,8]{0,1:T(8,128)S(1)}, u32[]{:S(2)}, u32[]{:S(2)}) collective-permute-start(f32[3,8]{0,1:T(8,128)S(1)} %get-tuple-element.79), channel_id=1, source_target_pairs={{32,0},{64,32},{96,64},{128,96},{160,128},{192,160},{224,192},{33,... | collective-permute-start | bytes 296 | tf_op jit(solution)/shard_map/ppermute | solution.py:44
  192.8 17.7 %all-to-all-start.1 = ((f32[32,3,4]{1,2,0:T(4,128)}), f32[32,3,4]{1,2,0:T(4,128)S(1)}, u32[]{:S(2)}, u32[]{:S(2)}) async-start(f32[32,3,4]{1,2,0:T(4,128)} %bitcast.45), calls=%async_computation.1 | async-start | bytes 131072 | tf_op jit(solution)/shard_map/all_to_all | solution.py:57
  202.5 4.3 %copy-start.4 = (f32[16,6,4096]{2,1,0:T(8,128)S(1)}, f32[16,6,4096]{2,1,0:T(8,128)}, u32[]{:S(2)}) copy-start(f32[16,6,4096]{2,1,0:T(8,128)} %copy.159) | copy-start | bytes 4718596
  210.5 113.4 %all-to-all-start.2 = ((f32[64,6,4096]{2,1,0:T(8,128)}), f32[64,6,4096]{2,1,0:T(8,128)}, u32[]{:S(2)}, u32[]{:S(2)}) async-start(f32[64,6,4096]{2,1,0:T(8,128)} %scatter_fusion), calls=%async_computation.2 | async-start | bytes 16777216 | tf_op jit(solution)/shard_map/all_to_all | solution.py:262
  (5 other events, 5.1 us)
where the time goes:
time: 336 us; the launch traced here: 330 us
  waiting for transfers between devices  106 us (32%)
  local copies, waits for them, and re-layouts  101 us (30%)
  starting transfers between devices  44 us (13%)
  matrix products  42.6 us (13%)
  other arithmetic  35.2 us (10%)
    all_to_all x1, waiting for transfers between devices, on_device(): lax.all_to_all(send_field, 'rve', split_axis=0, concat_axis=0, tiled=True)  102 us
    dot_general x8, matrix products, line_product(): jnp.einsum('ab,mbc->mac', table, field, precision=lax.Precision.HIGHEST)  27.4 us
    slice x4, local copies, waits for them, and re-layouts, green_apply(): entries = [polar[..., component, :] for component in range(6)]  18.6 us
    dot_general x4, matrix products, product(): jnp.dot(left, right, preferred_element_type=jnp.float32, precision=lax.Pr...  14.9 us
    unnamed x63, local copies, waits for them, and re-layouts  12.1 us
    ppermute x2, starting transfers between devices, extended_2(): before = lax.ppermute(last, axis, up)  10.4 us
    reshape x4, local copies, waits for them, and re-layouts, to_spectrum(): return (real_full.reshape(polar.shape), imag_full.reshape(polar.shape))  9.3 us
    another operation x4, local copies, waits for them, and re-layouts, green_apply(): return jnp.stack(result, axis=-2)  7.82 us
  transfers between devices with their start and end apart: 8, of which 3 were waited for; matrix products, arithmetic and copies ran while one was open for 50% of the time, Pallas kernels for 0%

commit v1 on v0

v1 whole, which is shorter than its diff:
```python
import functools
import math

import jax
import jax.numpy as jnp
import numpy as np
from jax import lax
from jax.experimental import pallas as pl
from jax.experimental.pallas import tpu as pltpu
from jax.sharding import PartitionSpec as P

RES = 16
PLANE = 256
LANES = 128
TILES = 32
COMPS = 6
HALF = 8
ROWS = COMPS * HALF
SPAN = 8 * HALF
MESH = pl.DeviceIdType.MESH
f32 = jnp.float32
bf16 = jnp.bfloat16
index_pairs = ((0, 0), (1, 1), (2, 2), (1, 2), (0, 2), (0, 1))
coef_rows = [(c, d) for c in range(6) for d in range(c, 6)]
coef_at = {}
for _at, (_c, _d) in enumerate(coef_rows):
    coef_at[(_c, _d)] = _at
    coef_at[(_d, _c)] = _at


def half_planes():
    own = [(0, 0), (0, 8), (8, 0), (8, 8)]
    pairs, seen = [], set(own)
    for y in range(RES):
        for z in range(RES):
            if (y, z) not in seen:
                seen.add((y, z))
                seen.add(((-y) % RES, (-z) % RES))
                pairs.append((y, z))
    lane_a = pairs + [(0, 0), (0, 8)]
    lane_b = pairs + [(8, 0), (8, 8)]
    return np.array(lane_a), np.array(lane_b), len(pairs)


def green_matrix(kx, ky, kz):
    def one(x, y, z):
        k = np.stack([x % RES, y % RES, z % RES]).astype(np.int64)
        xi = np.where(k < RES // 2, k, k - RES).astype(np.float64)
        size = np.sqrt((xi * xi).sum(0))
        n = np.where(size > 0, xi / np.where(size > 0, size, 1.0), 0.0)
        out = np.zeros((6, 6) + size.shape)
        for d, (i, j) in enumerate(index_pairs):
            t = np.zeros((3,) + size.shape)
            t[i] += n[j]
            if i != j:
                t[j] += n[i]
            s = (n * t).sum(0)
            weight = 1.0 if i == j else 2.0
            for c, (k_, h_) in enumerate(index_pairs):
                value = (n[k_] * t[h_] + n[h_] * t[k_]) / 2.2
                value = value - (2.2 / (1.1 * 3.3)) * n[k_] * n[h_] * s
                out[c, d] = value / weight
        return out

    return 0.5 * (one(kx, ky, kz) + one(-kx, -ky, -kz))


@functools.lru_cache(None)
def tables():
    lane_a, lane_b, count = half_planes()
    v = np.arange(PLANE)
    vy, vz = v // RES, v % RES
    angle = 2.0 * math.pi / RES

    def phase(lane):
        return angle * ((np.outer(vy, lane[:, 0]) + np.outer(vz, lane[:, 1])) % RES)

    paired = (np.arange(LANES) < count)[None, :]
    forward = np.concatenate(
        [np.cos(phase(lane_a)), np.where(paired, -np.sin(phase(lane_b)), np.cos(phase(lane_b)))], axis=1
    )
    coef = np.zeros((RES, 2, 24, LANES))
    for slot in range(RES):
        for part in range(2):
            ky, kz, kx, scale = [], [], [], []
            for lane in range(LANES):
                if lane < count:
                    y, z, x, weight = *lane_a[lane], slot, 2.0
                elif slot in (0, RES // 2):
                    y, z = lane_a[lane] if part == 0 else lane_b[lane]
                    x, weight = slot, 1.0
                else:
                    y, z = lane_a[lane] if slot < RES // 2 else lane_b[lane]
                    x, weight = (slot if slot < RES // 2 else RES - slot), 0.5
                ky.append(y), kz.append(z), kx.append(x), scale.append(weight / RES**3)
            matrix = green_matrix(np.array(kx), np.array(ky), np.array(kz)) * np.array(scale)
            for row, (c, d) in enumerate(coef_rows):
                coef[slot, part, row] = matrix[c, d]

    def split(table):
        high = jnp.asarray(table, f32).astype(bf16)
        low = (np.asarray(table, np.float64) - np.asarray(high).astype(np.float64)).astype(np.float32)
        return np.asarray(high), np.asarray(jnp.asarray(low).astype(bf16))

    with jax.ensure_compile_time_eval():
        fh, fl = split(forward)
        ih, il = split(forward.T)
    return np.stack([fh, fl, ih, il]), coef.astype(np.float32), count


def complex_mul(a, b):
    re, im = a
    cr, ci = b
    if abs(ci) < 1e-12 and abs(cr - 1) < 1e-12:
        return a
    if abs(cr) < 1e-12:
        return (im, -re) if ci < 0 else (-im, re)
    if abs(abs(cr) - abs(ci)) < 1e-12:
        h = abs(cr)
        sr, si = cr > 0, ci > 0
        if sr and not si:
            return (h * (re + im), h * (im - re))
        if not sr and not si:
            return (h * (im - re), -h * (re + im))
        if sr and si:
            return (h * (re - im), h * (im + re))
        return (-h * (re + im), h * (re - im))
    return (cr * re - ci * im, cr * im + ci * re)


def four_point(a, b, c, d, sign):
    s0 = (a[0] + c[0], a[1] + c[1])
    s1 = (a[0] - c[0], a[1] - c[1])
    s2 = (b[0] + d[0], b[1] + d[1])
    s3 = (b[0] - d[0], b[1] - d[1])
    turned = (s3[1], -s3[0]) if sign < 0 else (-s3[1], s3[0])
    return (
        (s0[0] + s2[0], s0[1] + s2[1]),
        (s1[0] + turned[0], s1[1] + turned[1]),
        (s0[0] - s2[0], s0[1] - s2[1]),
        (s1[0] - turned[0], s1[1] - turned[1]),
    )


def sixteen_point(values, sign):
    columns = []
    for r in range(4):
        out = four_point(values[r], values[r + 4], values[r + 8], values[r + 12], sign)
        columns.append(
            [
                complex_mul(out[k], (math.cos(2 * math.pi * r * k / 16), sign * math.sin(2 * math.pi * r * k / 16)))
                for k in range(4)
            ]
        )
    result = [None] * 16
    for k in range(4):
        out = four_point(columns[0][k], columns[1][k], columns[2][k], columns[3][k], sign)
        for m in range(4):
            result[k + 4 * m] = out[m]
    return result


def iota(shape, dim):
    return lax.broadcasted_iota(jnp.int32, shape, dim)


def sum_lanes(x):
    return jnp.sum(x, axis=1, keepdims=True)


def sum_rows(x):
    return jnp.sum(x, axis=0, keepdims=True)


def split_bf16(x):
    high = x.astype(bf16)
    low = (x - high.astype(f32)).astype(bf16)
    return high, low


def three_pass(high, low, table_high, table_low):
    def dot(a, b):
        return jnp.dot(a, b, preferred_element_type=f32)

    return dot(high, table_high) + (dot(low, table_high) + dot(high, table_low))


def main_kernel(
    count_paired, n_rve, n_mesh,
    disp_h, grads_h, weight_h, conn_h, halo_h, owner_h, sweeps_h, warm_h, moduli_h, plane_h, coef_h,
    nodal_o, stress_o, got2,
    warm_v, moduli_v, plane_v, coef_v, field, mod, tau_h, tau_l, spec, got1_a, got1_b, stage,
    tile_v, gathered, halo_out, halo_in, force_out, force_in, own_out, own_in,
    perm_v, perm_s, table_v, table_s, column_v,
    disp_s, grads_v, weight_v, conn_v, halo_v, owner_v, sweeps_v, small_sem,
    in_sem, idx_sem, gather_send, gather_recv, halo_send, halo_recv,
    send1, recv1, send2, recv2, fhalo_send, fhalo_recv, own_send, own_recv,
):
    me = lax.axis_index("rve")
    part = lax.axis_index("mesh")
    others = n_rve - 1
    got1 = (got1_a, got1_b)
    last_row = others * SPAN + HALF - 1
    has_below = part > 0
    has_above = part < n_mesh - 1

    small = [
        pltpu.make_async_copy(source, target, small_sem.at[at])
        for at, (source, target) in enumerate((
            (owner_h, owner_v), (sweeps_h, sweeps_v), (disp_h, disp_s), (halo_h, halo_v),
            (conn_h, conn_v), (grads_h, grads_v), (weight_h, weight_v),
        ))
    ]
    for load in small:
        load.start()

    def load_tile(t):
        at = pl.multiple_of(t * LANES, LANES)
        return pltpu.make_async_copy(
            warm_h.at[:, pl.ds(at, LANES)], warm_v.at[t, pl.ds(0, COMPS * 16), :], in_sem.at[0]
        )

    def start_tile(t, carry):
        load_tile(t).start()
        return carry

    lax.fori_loop(0, TILES, start_tile, 0)
    big_loads = [
        pltpu.make_async_copy(moduli_h, moduli_v, in_sem.at[1]),
        pltpu.make_async_copy(plane_h, plane_v, in_sem.at[2]),
        pltpu.make_async_copy(coef_h, coef_v, in_sem.at[3]),
    ]
    for load in big_loads:
        load.start()

    barrier = pltpu.get_barrier_semaphore()

    def greet(k, carry):
        pl.semaphore_signal(barrier, inc=1, device_id={"rve": lax.rem(me + k, n_rve)}, device_id_type=MESH)
        return carry

    lax.fori_loop(1, n_rve, greet, 0)

    @pl.when(has_below)
    def _():
        pl.semaphore_signal(barrier, inc=1, device_id={"mesh": part - 1}, device_id_type=MESH)

    @pl.when(has_above)
    def _():
        pl.semaphore_signal(barrier, inc=1, device_id={"mesh": part + 1}, device_id_type=MESH)

    for load in small:
        load.wait()

    owner_row = owner_v[...].astype(f32)
    sub16, lane16 = iota((16, 16), 0), iota((16, 16), 1)
    owner_col = sum_lanes(jnp.where(sub16 == lane16, jnp.broadcast_to(owner_row, (16, 16)), 0.0))
    place = 0.5 * sum_rows(jnp.where(owner_col < owner_row, 1.0, 0.0))
    rank = sum_rows(jnp.where((owner_col == owner_row) & (sub16 < lane16), 1.0, 0.0))
    slot_row = 8.0 * rank + place
    chosen = jnp.where(slot_row == sub16.astype(f32), 1.0, 0.0)
    perm_col = sum_lanes(chosen * lane16.astype(f32))
    perm_v[...] = jnp.broadcast_to(perm_col, (16, LANES)).astype(jnp.int32)
    count_col = sum_lanes(chosen * sweeps_v[...].astype(f32))
    load_perm = pltpu.make_async_copy(perm_v, perm_s, idx_sem.at[0])
    load_perm.start()

    lane_row = iota((1, LANES), 1).astype(f32)
    sends_row = 0.5 * sum_rows(jnp.where(owner_col == lane_row, 1.0, 0.0))
    sub4, lane4 = iota((4, LANES), 0), iota((4, LANES), 1)
    tile = jnp.where(sub4 == 3, sends_row, 0.0)
    for i in range(3):
        for node in range(4):
            tile = jnp.where((sub4 == i) & (lane4 == 4 * me + node), disp_s[i, node], tile)
    tile_v[...] = tile
    gathered[me] = tile

    extra = jnp.where(has_below, 1, 0) + jnp.where(has_above, 1, 0)
    pl.semaphore_wait(barrier, others + extra)

    def to_all(source, target, send, recv):
        def body(k, carry):
            to = lax.rem(me + k, n_rve)
            pltpu.make_async_remote_copy(
                source, target, send, recv, device_id={"rve": to}, device_id_type=MESH
            ).start()
            return carry

        lax.fori_loop(1, n_rve, body, 0)

    def wait_bytes(view, sem):
        pltpu.make_async_copy(view, view, sem).wait()

    to_all(tile_v, gathered.at[me], gather_send, gather_recv)

    load_perm.wait()
    big_loads[0].wait()

    wait_bytes(warm_v.at[:, pl.ds(0, COMPS * 16), :], in_sem.at[0])
    for half in range(2):
        for pos in range(HALF):
            point = jnp.clip(perm_s[half * HALF + pos, 0], 0, 15)

            def place_tile(t, carry):
                at = pl.multiple_of(t * LANES, LANES)
                field[half, t, pl.ds(pos, COMPS, stride=HALF), :] = warm_v[t, pl.ds(point, COMPS, stride=16), :]
                mod[half, t, pl.ds(pos, 2, stride=HALF), :] = moduli_v[point, :, pl.ds(at, LANES)]
                return carry

            lax.fori_loop(0, TILES, place_tile, 0)

    def mean_of(half):
        def body(t, sums):
            return tuple(sums[c] + field[half, t, c * HALF : (c + 1) * HALF, :] for c in range(COMPS))

        sums = lax.fori_loop(0, TILES, body, tuple(jnp.zeros((HALF, LANES), f32) for _ in range(COMPS)))
        return [sum_lanes(s) * (1.0 / 4096.0) for s in sums]

    means = [mean_of(0), mean_of(1)]

    wait_bytes(gathered.at[pl.ds(0, others)], gather_recv)
    moved = jnp.sum(gathered[...], axis=0)
    lane8, sub8 = iota((HALF, LANES), 1).astype(f32), iota((HALF, LANES), 0).astype(f32)
    eye8 = iota((HALF, HALF), 0) == iota((HALF, HALF), 1)
    halo_rows = halo_v[...].astype(f32)
    halo_hot = []
    for side in range(2):
        col = sum_lanes(jnp.where(eye8, jnp.broadcast_to(halo_rows[side : side + 1], (HALF, HALF)), 0.0))
        halo_hot.append(jnp.where(col == lane8, 1.0, 0.0))
    out_tile = jnp.zeros((HALF, LANES), f32)
    for side in range(2):
        for i in range(3):
            col = sum_lanes(halo_hot[side] * moved[i : i + 1])
            out_tile = jnp.where(lane8 == 3 * side + i, col, out_tile)
    halo_out[...] = out_tile

    def swap_halo(source, target, send, recv):
        @pl.when(has_below)
        def _():
            pltpu.make_async_remote_copy(
                source, target.at[1], send.at[0], recv.at[1], device_id={"mesh": part - 1}, device_id_type=MESH
            ).start()

        @pl.when(has_above)
        def _():
            pltpu.make_async_remote_copy(
                source, target.at[0], send.at[1], recv.at[0], device_id={"mesh": part + 1}, device_id_type=MESH
            ).start()

    def take_halo(source, target, recv):
        @pl.when(has_below)
        def _():
            wait_bytes(target.at[0], recv.at[0])

        @pl.when(jnp.logical_not(has_below))
        def _():
            target[0] = jnp.zeros((HALF, LANES), f32)

        @pl.when(has_above)
        def _():
            wait_bytes(target.at[1], recv.at[1])

        @pl.when(jnp.logical_not(has_above))
        def _():
            target[1] = jnp.zeros((HALF, LANES), f32)

    swap_halo(halo_out, halo_in, halo_send, halo_recv)

    sends = jnp.concatenate([gathered[s, 3:4] for s in range(n_rve)], axis=0)
    lower = jnp.where(iota((n_rve, n_rve), 1) < iota((n_rve, n_rve), 0), 1.0, 0.0).astype(bf16)
    upper = jnp.where(iota((LANES, LANES), 0) < iota((LANES, LANES), 1), 1.0, 0.0).astype(bf16)
    sends_b = sends.astype(bf16)
    order = jnp.dot(lower, sends_b, preferred_element_type=f32)
    places = jnp.dot(sends_b, upper, preferred_element_type=f32)
    rows_at = iota((n_rve, LANES), 0).astype(f32) * float(SPAN) + places
    table = jnp.zeros((HALF, LANES), f32)
    for k in range(HALF):
        row = sum_rows(jnp.where((sends > 0.5) & (order == float(k)), rows_at, 0.0))
        table = jnp.where(sub8 == float(k), row, table)
    table_v[...] = table.astype(jnp.int32)
    load_table = pltpu.make_async_copy(table_v, table_s, idx_sem.at[1])
    load_table.start()

    conn_rows = conn_v[...].astype(f32)
    own_hot, far_hot = [], []
    for e in range(2):
        col = sum_lanes(jnp.where(eye8, jnp.broadcast_to(conn_rows[e : e + 1], (HALF, HALF)), 0.0))
        own_hot.append(jnp.where(col == lane8, 1.0, 0.0))
        far_hot.append(jnp.where(col - float(LANES) == lane8, 1.0, 0.0))
    first_element = iota((HALF, 16), 1) < 8

    take_halo(halo_out, halo_in, halo_recv)
    below, above = halo_in[0], halo_in[1]
    spread_disp = []
    for i in range(3):
        far = sum_rows(jnp.where(lane8 == sub8, below[:, 3 + i : 4 + i], 0.0))
        far = far + sum_rows(jnp.where(lane8 == sub8 + 8.0, above[:, i : i + 1], 0.0))
        cols = [sum_lanes(own_hot[e] * moved[i : i + 1] + far_hot[e] * far) for e in range(2)]
        spread_disp.append(jnp.where(first_element, cols[0], cols[1]))
    grads = [grads_v[j] for j in range(3)]
    g = [[sum_rows(spread_disp[i] * grads[j]) for j in range(3)] for i in range(3)]
    macro = [
        g[0][0], g[1][1], g[2][2],
        (g[1][2] + g[2][1]) * 0.5, (g[0][2] + g[2][0]) * 0.5, (g[0][1] + g[1][0]) * 0.5,
    ]
    macro_cols = [sum_lanes(chosen * row) for row in macro]
    for c in range(COMPS):
        for half in range(2):
            col = macro_cols[c][half * HALF : (half + 1) * HALF]
            column_v[half, 0, c] = jnp.broadcast_to(col - means[half][c], (HALF, LANES))
            column_v[half, 1, c] = jnp.broadcast_to(col, (HALF, LANES))
    for half in range(2):
        column_v[half, 2, 0] = jnp.broadcast_to(count_col[half * HALF : (half + 1) * HALF], (HALF, LANES))

    big_loads[1].wait()
    big_loads[2].wait()
    odd_lane = iota((HALF, LANES), 1) >= count_paired

    def sweep(half, number):
        def polarize(u, carry):
            for b in range(2):
                cats = [[] for _ in range(COMPS)]
                for step in range(2):
                    t = (2 * u + step) * 2 + b
                    eps = [field[half, t, c * HALF : (c + 1) * HALF, :] for c in range(COMPS)]
                    if number == 0:
                        eps = [eps[c] + column_v[half, 0, c] for c in range(COMPS)]
                    lam = mod[half, t, 0:HALF, :] - 1.1
                    shear = 2.0 * mod[half, t, HALF : 2 * HALF, :] - 2.2
                    pressure = lam * (eps[0] + eps[1] + eps[2])
                    double = shear + shear
                    for c in range(3):
                        cats[c].append(shear * eps[c] + pressure)
                    for c in range(3, 6):
                        cats[c].append(double * eps[c])
                for c in range(COMPS):
                    high, low = split_bf16(jnp.concatenate(cats[c], axis=0))
                    at = pl.multiple_of(u * 16, 16)
                    tau_h[c, pl.ds(at, 16), b * LANES : (b + 1) * LANES] = high
                    tau_l[c, pl.ds(at, 16), b * LANES : (b + 1) * LANES] = low
            return carry

        lax.fori_loop(0, 8, polarize, 0)

        def forward(c, carry):
            planed = three_pass(tau_h[c], tau_l[c], plane_v[0], plane_v[1])
            values = [
                (planed[x * HALF : (x + 1) * HALF, :LANES], planed[x * HALF : (x + 1) * HALF, LANES:])
                for x in range(RES)
            ]
            z = sixteen_point(values, -1)
            for k in range(1, 8):
                a, b = z[k], z[RES - k]
                z[k] = (jnp.where(odd_lane, a[0] + b[0], a[0]), jnp.where(odd_lane, a[1] - b[1], a[1]))
                z[RES - k] = (jnp.where(odd_lane, a[1] + b[1], b[0]), jnp.where(odd_lane, b[0] - a[0], b[1]))
            for k in range(RES):
                spec[k, 0, c] = z[k][0]
                spec[k, 1, c] = z[k][1]
            return carry

        lax.fori_loop(0, COMPS, forward, 0)

        def green(k, carry):
            for part_at in range(2):
                ins = [spec[k, part_at, c] for c in range(COMPS)]
                rows = [coef_v[k, part_at, r : r + 1, :] for r in range(len(coef_rows))]
                for c in range(COMPS):
                    total = rows[coef_at[(c, 0)]] * ins[0]
                    for d in range(1, COMPS):
                        total = total + rows[coef_at[(c, d)]] * ins[d]
                    spec[k, part_at, c] = total
            return carry

        lax.fori_loop(0, RES, green, 0)

        def backward(c, carry):
            z = [(spec[k, 0, c], spec[k, 1, c]) for k in range(RES)]
            for k in range(1, 8):
                a, b = z[k], z[RES - k]
                z[k] = (jnp.where(odd_lane, a[0] - b[1], a[0]), jnp.where(odd_lane, a[1] + b[0], a[1]))
                z[RES - k] = (jnp.where(odd_lane, a[0] + b[1], b[0]), jnp.where(odd_lane, b[0] - a[1], b[1]))
            values = sixteen_point(z, 1)
            lined = jnp.concatenate(
                [
                    jnp.concatenate([values[x][0] for x in range(RES)], axis=0),
                    jnp.concatenate([values[x][1] for x in range(RES)], axis=0),
                ],
                axis=1,
            )
            high, low = split_bf16(lined)
            fluct = three_pass(high, low, plane_v[2], plane_v[3])
            level = column_v[half, 1, c]
            again = column_v[half, 2, 0] > float(number) + 0.5
            at = pl.multiple_of(c * HALF, HALF)
            for x in range(RES):
                for b in range(2):
                    new = level - fluct[x * HALF : (x + 1) * HALF, b * LANES : (b + 1) * LANES]
                    t = 2 * x + b
                    if number > 0:
                        new = jnp.where(again, new, field[half, t, pl.ds(at, HALF), :])
                    field[half, t, pl.ds(at, HALF), :] = new
            return carry

        lax.fori_loop(0, COMPS, backward, 0)

    def mean_stress(half):
        def body(t, sums):
            eps = [field[half, t, c * HALF : (c + 1) * HALF, :] for c in range(COMPS)]
            lam = mod[half, t, 0:HALF, :]
            shear = mod[half, t, HALF : 2 * HALF, :]
            new = [sums[c] + shear * eps[c] for c in range(COMPS)]
            return (*new, sums[6] + lam * (eps[0] + eps[1] + eps[2]))

        sums = lax.fori_loop(0, TILES, body, tuple(jnp.zeros((HALF, LANES), f32) for _ in range(7)))
        result = []
        for c in range(COMPS):
            total = 2.0 * sums[c]
            if c < 3:
                total = total + sums[6]
            result.append(sum_lanes(total) * (1.0 / 4096.0))
        return result

    def send_spread(half):
        rows = pl.multiple_of(me * SPAN, SPAN)
        got1[half][pl.ds(rows, ROWS), :] = field[half, me, pl.ds(0, ROWS), :]

        def body(k, carry):
            to = lax.rem(me + k, n_rve)
            pltpu.make_async_remote_copy(
                field.at[half, to, pl.ds(0, ROWS), :], got1[half].at[pl.ds(rows, ROWS), :], send1.at[half], recv1.at[half],
                device_id={"rve": to}, device_id_type=MESH,
            ).start()
            return carry

        lax.fori_loop(1, n_rve, body, 0)

    def send_owned(half):
        wait_bytes(got2.at[half, pl.ds(0, others)], recv1.at[half])

        def body(k, carry):
            to = lax.rem(me + k, n_rve)
            for at in range(HALF):
                row = jnp.clip(table_s[at, to], 0, last_row)
                stage[half, to, pl.ds(at, COMPS, stride=HALF), :] = got1[half][
                    pl.ds(row, COMPS, stride=HALF), :
                ]

            @pl.when(k > 0)
            def _():
                pltpu.make_async_remote_copy(
                    stage.at[half, to, pl.ds(0, ROWS), :], got2.at[half, me], send2.at[half], recv2.at[half],
                    device_id={"rve": to}, device_id_type=MESH,
                ).start()

            return carry

        lax.fori_loop(1, n_rve, body, 0)
        body(0, 0)
        keep = pltpu.make_async_copy(stage.at[half, me, pl.ds(0, ROWS), :], got2.at[half, me], in_sem.at[4 + half])
        keep.start()
        return keep

    load_table.wait()
    sweep(0, 0)
    sweep(0, 1)
    send_spread(0)
    stress = [mean_stress(0)]
    sweep(1, 0)
    keep0 = send_owned(0)
    sweep(1, 1)
    send_spread(1)
    stress.append(mean_stress(1))

    weights = weight_v[...]
    sigma = []
    for c in range(COMPS):
        col = jnp.concatenate([stress[0][c], stress[1][c]], axis=0)
        row = sum_rows(chosen * col)
        stress_o[c : c + 1, :] = row
        sigma.append(row * weights)
    grid = ((0, 5, 4), (5, 1, 3), (4, 3, 2))
    force_tile = jnp.zeros((HALF, LANES), f32)
    own_rows = []
    for i in range(3):
        point_force = sigma[grid[i][0]] * grads[0] + sigma[grid[i][1]] * grads[1] + sigma[grid[i][2]] * grads[2]
        cols = [
            sum_lanes(jnp.where(first_element, point_force, 0.0)),
            sum_lanes(jnp.where(first_element, 0.0, point_force)),
        ]
        own_rows.append(sum_rows(own_hot[0] * cols[0] + own_hot[1] * cols[1]))
        far = sum_rows(far_hot[0] * cols[0] + far_hot[1] * cols[1])
        force_tile = jnp.where(sub8 == float(i), far, force_tile)
    force_out[...] = force_tile
    swap_halo(force_out, force_in, fhalo_send, fhalo_recv)
    keep1 = send_owned(1)
    take_halo(force_out, force_in, fhalo_recv)
    below, above = force_in[0], force_in[1]
    own_tile = jnp.zeros((4, LANES), f32)
    for i in range(3):
        low = sum_lanes(jnp.where(lane8 == sub8 + 8.0, below[i : i + 1], 0.0))
        high = sum_lanes(jnp.where(lane8 == sub8, above[i : i + 1], 0.0))
        row = own_rows[i] + sum_rows(halo_hot[0] * low + halo_hot[1] * high)
        own_tile = jnp.where(sub4 == i, row, own_tile)
    own_out[...] = own_tile
    own_in[me] = own_tile
    to_all(own_out, own_in.at[me], own_send, own_recv)
    wait_bytes(own_in.at[pl.ds(0, others)], own_recv)
    total = jnp.sum(own_in[...], axis=0)
    mine = jnp.zeros((4, LANES), f32)
    for node in range(4):
        mine = jnp.where(lane4 == node, sum_lanes(jnp.where(lane4 == 4 * me + node, total, 0.0)), mine)
    nodal_o[...] = mine[:3, :4]

    keep0.wait()
    keep1.wait()
    for half in range(2):
        wait_bytes(got2.at[half, pl.ds(0, others)], recv2.at[half])
    wait_bytes(gathered.at[pl.ds(0, others)], gather_send)
    wait_bytes(own_in.at[pl.ds(0, others)], own_send)
    for half in range(2):
        wait_bytes(got2.at[half, pl.ds(0, others)], send1.at[half])
        wait_bytes(got2.at[half, pl.ds(0, others)], send2.at[half])
    for send, source in ((halo_send, halo_out), (fhalo_send, force_out)):
        @pl.when(has_below)
        def _(send=send, source=source):
            wait_bytes(source, send.at[0])

        @pl.when(has_above)
        def _(send=send, source=source):
            wait_bytes(source, send.at[1])


def lay_out_kernel(got_h, nodal_ref, stress_ref, out_h, nodal_o, stress_o, taken, mixed, in_sem, out_sem):
    parts = mixed.shape[0]
    group = TILES // parts

    def copy_in(at):
        return pltpu.make_async_copy(got_h.at[:, pl.ds(at * group, group)], taken.at[at], in_sem.at[at])

    def copy_out(at):
        return pltpu.make_async_copy(
            mixed.at[at], out_h.at[:, pl.ds(at * group * LANES, group * LANES)], out_sem.at[at]
        )

    for at in range(parts):
        copy_in(at).start()
    nodal_o[...] = nodal_ref[...]
    stress_o[...] = stress_ref[...]
    for at in range(parts):
        copy_in(at).wait()
        for t in range(group):
            for c in range(COMPS):
                first, second = (taken[at, half, t, c * HALF : (c + 1) * HALF, :] for half in range(2))
                pair = jnp.concatenate([first[:, None], second[:, None]], axis=1).reshape(2 * HALF, LANES)
                mixed[at, 2 * HALF * c : 2 * HALF * (c + 1), t * LANES : (t + 1) * LANES] = pair
        copy_out(at).start()
    for at in range(parts):
        copy_out(at).wait()


def lay_out(got, nodal, stress):
    parts = 8
    vmem = pl.BlockSpec(memory_space=pltpu.VMEM)
    hbm = pl.BlockSpec(memory_space=pltpu.HBM)
    return pl.pallas_call(
        lay_out_kernel,
        in_specs=[hbm, vmem, vmem],
        out_specs=[hbm, vmem, vmem],
        out_shape=[
            jax.ShapeDtypeStruct((2 * ROWS, TILES * LANES), f32),
            jax.ShapeDtypeStruct(nodal.shape, f32),
            jax.ShapeDtypeStruct(stress.shape, f32),
        ],
        scratch_shapes=[
            pltpu.VMEM((parts, 2, TILES // parts, ROWS, LANES), f32),
            pltpu.VMEM((parts, 2 * ROWS, TILES // parts * LANES), f32),
            pltpu.SemaphoreType.DMA((parts,)),
            pltpu.SemaphoreType.DMA((parts,)),
        ],
        compiler_params=pltpu.CompilerParams(vmem_limit_bytes=63 * 1024 * 1024),
        name="lay_out",
    )(got, nodal, stress)


def solution(mesh):
    n_rve, n_mesh = mesh.shape["rve"], mesh.shape["mesh"]
    planes, coef, count_paired = tables()

    def on_device(displacement, shape_grads, point_weights, conn, halo_nodes, warm_strain, moduli, owner, sweeps):
        points, voxels = warm_strain.shape[0], warm_strain.shape[2]
        warm = warm_strain.transpose(1, 0, 2).reshape(COMPS * points, voxels)
        vmem = pl.BlockSpec(memory_space=pltpu.VMEM)
        hbm = pl.BlockSpec(memory_space=pltpu.HBM)
        dma = pltpu.SemaphoreType.DMA
        scratch = [
            pltpu.VMEM((TILES, 8 * points, LANES), f32),
            pltpu.VMEM((points, 2, voxels), f32),
            pltpu.VMEM(planes.shape, bf16),
            pltpu.VMEM(coef.shape, f32),
            pltpu.VMEM((2, TILES, SPAN, LANES), f32),
            pltpu.VMEM((2, TILES, SPAN, LANES), f32),
            pltpu.VMEM((COMPS, RES * HALF, PLANE), bf16),
            pltpu.VMEM((COMPS, RES * HALF, PLANE), bf16),
            pltpu.VMEM((RES, 2, COMPS, HALF, LANES), f32),
            pltpu.VMEM((n_rve * SPAN, LANES), f32),
            pltpu.VMEM((n_rve * SPAN, LANES), f32),
            pltpu.VMEM((2, n_rve, SPAN, LANES), f32),
            pltpu.VMEM((4, LANES), f32),
            pltpu.VMEM((n_rve, 4, LANES), f32),
            pltpu.VMEM((HALF, LANES), f32),
            pltpu.VMEM((2, HALF, LANES), f32),
            pltpu.VMEM((HALF, LANES), f32),
            pltpu.VMEM((2, HALF, LANES), f32),
            pltpu.VMEM((4, LANES), f32),
            pltpu.VMEM((n_rve, 4, LANES), f32),
            pltpu.VMEM((16, LANES), jnp.int32),
            pltpu.SMEM((16, LANES), jnp.int32),
            pltpu.VMEM((HALF, LANES), jnp.int32),
            pltpu.SMEM((HALF, LANES), jnp.int32),
            pltpu.VMEM((2, 3, COMPS, HALF, LANES), f32),
            pltpu.SMEM((3, 4), f32),
            pltpu.VMEM(shape_grads.shape, f32),
            pltpu.VMEM((1, points), f32),
            pltpu.VMEM((2, 8), jnp.int32),
            pltpu.VMEM((2, 8), jnp.int32),
            pltpu.VMEM((1, points), jnp.int32),
            pltpu.VMEM((1, points), jnp.int32),
            dma((7,)),
            dma((6,)), dma((2,)), dma, dma, dma((2,)), dma((2,)),
            dma((2,)), dma((2,)), dma((2,)), dma((2,)), dma((2,)), dma((2,)), dma, dma,
        ]
        nodal, stress, got = pl.pallas_call(
            functools.partial(main_kernel, count_paired, n_rve, n_mesh),
            in_specs=[hbm] * 11,
            out_specs=[vmem, vmem, hbm],
            out_shape=[
                jax.ShapeDtypeStruct((3, 4), f32),
                jax.ShapeDtypeStruct((COMPS, points), f32),
                jax.ShapeDtypeStruct((2, n_rve, ROWS, LANES), f32),
            ],
            scratch_shapes=scratch,
            compiler_params=pltpu.CompilerParams(
                collective_id=0, has_side_effects=True, vmem_limit_bytes=63 * 1024 * 1024
            ),
            name="solve_and_exchange",
        )(
            displacement, shape_grads, point_weights.reshape(1, points), conn.T, halo_nodes,
            owner.reshape(1, points), sweeps.reshape(1, points), warm, moduli,
            jnp.asarray(planes), jnp.asarray(coef),
        )
        micro, nodal, stress = lay_out(got, nodal, stress)
        micro = micro.reshape(COMPS, points, voxels).transpose(1, 0, 2)
        return nodal, stress, micro

    both = ("mesh", "rve")
    in_specs = (
        P(None, both), P(None, None, both), P(both), P(None, both), P(None, "mesh"),
        P(both, None, None), P(both, None, None), P(both), P(both),
    )
    out_specs = (P(None, both), P(None, both), P(both, None, None))
    return jax.shard_map(on_device, mesh=mesh, in_specs=in_specs, out_specs=out_specs, check_vma=False)
```

time: 336 us -> 74.8 us (0.22); the launches traced: 330 us -> 74.4 us
  waiting for transfers between devices: 106 us -> 0 us
  local copies, waits for them, and re-layouts: 101 us -> 0 us
  Pallas kernels: 0 us -> 73.8 us
  starting transfers between devices: 44 us -> 0 us
  matrix products: 42.6 us -> 0 us
  other arithmetic: 35.2 us -> 0 us
    all_to_all x4 -> x0, waiting for transfers between devices: 102 us -> none  [the longest x1 102 us: on_device(): lax.all_to_all(send_field, 'rve', split_axis=0, concat_axis=0, tiled=True)]
    pallas_call x0 -> x2, Pallas kernels: none -> 73.8 us  [the longest x1 69.4 us: on_device(): pl.pallas_call(functools.partial(main_kernel, count_paired, n_rve, n_mesh...]
    dot_general x14 -> x0, matrix products: 42.6 us -> none  [the longest x8 27.4 us: line_product(): jnp.einsum('ab,mbc->mac', table, field, precision=lax.Precision.HIGHEST)]
    all_to_all x4 -> x0, starting transfers between devices: 29.6 us -> none  [the longest x1 7.52 us: on_device(): lax.all_to_all(send_field, 'rve', split_axis=0, concat_axis=0, tiled=True)]
    reshape x13 -> x0, local copies, waits for them, and re-layouts: 21 us -> none  [the longest x4 9.3 us: to_spectrum(): return (real_full.reshape(polar.shape), imag_full.reshape(polar.shape))]
    slice x8 -> x0, local copies, waits for them, and re-layouts: 19.8 us -> none  [the longest x4 18.6 us: green_apply(): entries = [polar[..., component, :] for component in range(6)]]
    ppermute x4 -> x0, starting transfers between devices: 14.3 us -> none  [the longest x2 10.4 us: extended_2(): before = lax.ppermute(last, axis, up)]
    unnamed x63 -> x0, local copies, waits for them, and re-layouts: 12.1 us -> none
  transfers between devices with their start and end apart: 8 -> 0, of which waited for: 3 -> 0; matrix products, arithmetic and copies ran while one was open for 50% -> 0% of each run, Pallas kernels for 0% -> 0%
where the time goes in v1:
time: 74.8 us; the launch traced here: 74.4 us
  Pallas kernels  73.8 us (99%)
    pallas_call x1, Pallas kernels, on_device(): pl.pallas_call(functools.partial(main_kernel, count_paired, n_rve, n_mesh...  69.4 us
    pallas_call x1, Pallas kernels, lay_out(): pl.pallas_call(lay_out_kernel, in_specs=[hbm, vmem, vmem], out_specs=[hbm...  4.38 us

profile of v1, /device:TPU:96, one launch (start us, length us, event | category | flops | bytes accessed | tf_op | source)
XLA Modules:
  0.0 74.4 jit_solution(3413798060756211623)
XLA Ops:
  0.6 69.4 %solve_and_exchange.1 = (f32[3,4]{1,0:T(4,128)}, f32[6,16]{1,0:T(8,128)}, f32[2,32,48,128]{3,2,1,0:T(8,128)}) custom-call(f32[3,4]{1,0:T(4,128)} %disp_h.1, f32[3,8,16]{2,1,0:T(8,128)} %grads_h.1, f32[1,16]{1,0:T(1,128)} %bitcast.12, s32[2,8]{1,0:T(2,128)} %bitcast.11, s32[2,8]{1,0:T(2,128)} %halo_h.1, s32[1,16]{1,0:T(1,128)} %bitcast.13, s32[1,16]{1,0:T(1,128)} %bitcast.14, ...), custom_call_target="tpu_custom_call" | custom-call | tf_op jit(solution)/shard_map/solve_and_exchange/pallas_call | solution.py:732
  70.0 4.4 %lay_out.1 = (f32[96,4096]{1,0:T(8,128)}, f32[3,4]{1,0:T(4,128)}, f32[6,16]{1,0:T(8,128)}) custom-call(f32[2,32,48,128]{3,2,1,0:T(8,128)} %get-tuple-element.9.got_h, f32[3,4]{1,0:T(4,128)} %get-tuple-element.10.nodal_ref, f32[6,16]{1,0:T(8,128)} %get-tuple-element.11.stress_ref), custom_call_target="tpu_custom_call" | custom-call | tf_op jit(solution)/shard_map/lay_out/pallas_call | solution.py:665

commit v2 on v1

--- a/solution.py
+++ b/solution.py
@@ -297,26 +297,30 @@
     big_loads[0].wait()
 
     wait_bytes(warm_v.at[:, pl.ds(0, COMPS * 16), :], in_sem.at[0])
-    for half in range(2):
-        for pos in range(HALF):
-            point = jnp.clip(perm_s[half * HALF + pos, 0], 0, 15)
-
-            def place_tile(t, carry):
-                at = pl.multiple_of(t * LANES, LANES)
-                field[half, t, pl.ds(pos, COMPS, stride=HALF), :] = warm_v[t, pl.ds(point, COMPS, stride=16), :]
-                mod[half, t, pl.ds(pos, 2, stride=HALF), :] = moduli_v[point, :, pl.ds(at, LANES)]
-                return carry
-
-            lax.fori_loop(0, TILES, place_tile, 0)
-
-    def mean_of(half):
-        def body(t, sums):
-            return tuple(sums[c] + field[half, t, c * HALF : (c + 1) * HALF, :] for c in range(COMPS))
-
-        sums = lax.fori_loop(0, TILES, body, tuple(jnp.zeros((HALF, LANES), f32) for _ in range(COMPS)))
-        return [sum_lanes(s) * (1.0 / 4096.0) for s in sums]
-
-    means = [mean_of(0), mean_of(1)]
+    places_at = [
+        (half, pos, jnp.clip(perm_s[half * HALF + pos, 0], 0, 15)) for half in range(2) for pos in range(HALF)
+    ]
+
+    def place_tile(t, carry):
+        at = pl.multiple_of(t * LANES, LANES)
+        for half, pos, point in places_at:
+            field[half, t, pl.ds(pos, COMPS, stride=HALF), :] = warm_v[t, pl.ds(point, COMPS, stride=16), :]
+            mod[half, t, pl.ds(pos, 2, stride=HALF), :] = moduli_v[point, :, pl.ds(at, LANES)]
+        return carry
+
+    lax.fori_loop(0, TILES, place_tile, 0)
+
+    def add_up(t, sums):
+        return tuple(
+            sums[half * COMPS + c] + field[half, t, c * HALF : (c + 1) * HALF, :]
+            for half in range(2)
+            for c in range(COMPS)
+        )
+
+    sums = lax.fori_loop(
+        0, TILES, add_up, tuple(jnp.zeros((HALF, LANES), f32) for _ in range(2 * COMPS)), unroll=4
+    )
+    means = [[sum_lanes(sums[half * COMPS + c]) * (1.0 / 4096.0) for c in range(COMPS)] for half in range(2)]
 
     wait_bytes(gathered.at[pl.ds(0, others)], gather_recv)
     moved = jnp.sum(gathered[...], axis=0)
@@ -440,7 +444,7 @@
                     tau_l[c, pl.ds(at, 16), b * LANES : (b + 1) * LANES] = low
             return carry
 
-        lax.fori_loop(0, 8, polarize, 0)
+        lax.fori_loop(0, 8, polarize, 0, unroll=2)
 
         def forward(c, carry):
             planed = three_pass(tau_h[c], tau_l[c], plane_v[0], plane_v[1])
@@ -458,7 +462,7 @@
                 spec[k, 1, c] = z[k][1]
             return carry
 
-        lax.fori_loop(0, COMPS, forward, 0)
+        lax.fori_loop(0, COMPS, forward, 0, unroll=2)
 
         def green(k, carry):
             for part_at in range(2):
@@ -471,7 +475,7 @@
                     spec[k, part_at, c] = total
             return carry
 
-        lax.fori_loop(0, RES, green, 0)
+        lax.fori_loop(0, RES, green, 0, unroll=2)
 
         def backward(c, carry):
             z = [(spec[k, 0, c], spec[k, 1, c]) for k in range(RES)]
@@ -501,7 +505,7 @@
                     field[half, t, pl.ds(at, HALF), :] = new
             return carry
 
-        lax.fori_loop(0, COMPS, backward, 0)
+        lax.fori_loop(0, COMPS, backward, 0, unroll=2)
 
     def mean_stress(half):
         def body(t, sums):
@@ -511,7 +515,7 @@
             new = [sums[c] + shear * eps[c] for c in range(COMPS)]
             return (*new, sums[6] + lam * (eps[0] + eps[1] + eps[2]))
 
-        sums = lax.fori_loop(0, TILES, body, tuple(jnp.zeros((HALF, LANES), f32) for _ in range(7)))
+        sums = lax.fori_loop(0, TILES, body, tuple(jnp.zeros((HALF, LANES), f32) for _ in range(7)), unroll=4)
         result = []
         for c in range(COMPS):
             total = 2.0 * sums[c]
@@ -592,7 +596,6 @@
         force_tile = jnp.where(sub8 == float(i), far, force_tile)
     force_out[...] = force_tile
     swap_halo(force_out, force_in, fhalo_send, fhalo_recv)
-    keep1 = send_owned(1)
     take_halo(force_out, force_in, fhalo_recv)
     below, above = force_in[0], force_in[1]
     own_tile = jnp.zeros((4, LANES), f32)
@@ -604,6 +607,7 @@
     own_out[...] = own_tile
     own_in[me] = own_tile
     to_all(own_out, own_in.at[me], own_send, own_recv)
+    keep1 = send_owned(1)
     wait_bytes(own_in.at[pl.ds(0, others)], own_recv)
     total = jnp.sum(own_in[...], axis=0)
     mine = jnp.zeros((4, LANES), f32)
@@ -631,15 +635,15 @@
 
 
 def lay_out_kernel(got_h, nodal_ref, stress_ref, out_h, nodal_o, stress_o, taken, mixed, in_sem, out_sem):
-    parts = mixed.shape[0]
+    parts = taken.shape[0]
     group = TILES // parts
 
     def copy_in(at):
         return pltpu.make_async_copy(got_h.at[:, pl.ds(at * group, group)], taken.at[at], in_sem.at[at])
 
-    def copy_out(at):
+    def copy_out(t):
         return pltpu.make_async_copy(
-            mixed.at[at], out_h.at[:, pl.ds(at * group * LANES, group * LANES)], out_sem.at[at]
+            mixed.at[t, pl.ds(0, 2 * ROWS), :], out_h.at[:, pl.ds(t * LANES, LANES)], out_sem.at[t]
         )
 
     for at in range(parts):
@@ -650,12 +654,13 @@
         copy_in(at).wait()
         for t in range(group):
             for c in range(COMPS):
-                first, second = (taken[at, half, t, c * HALF : (c + 1) * HALF, :] for half in range(2))
-                pair = jnp.concatenate([first[:, None], second[:, None]], axis=1).reshape(2 * HALF, LANES)
-                mixed[at, 2 * HALF * c : 2 * HALF * (c + 1), t * LANES : (t + 1) * LANES] = pair
-        copy_out(at).start()
-    for at in range(parts):
-        copy_out(at).wait()
+                for half in range(2):
+                    mixed[at * group + t, pl.ds(2 * HALF * c + half, HALF, stride=2), :] = taken[
+                        at, half, t, c * HALF : (c + 1) * HALF, :
+                    ]
+            copy_out(at * group + t).start()
+    for t in range(TILES):
+        copy_out(t).wait()
 
 
 def lay_out(got, nodal, stress):
@@ -673,9 +678,9 @@
         ],
         scratch_shapes=[
             pltpu.VMEM((parts, 2, TILES // parts, ROWS, LANES), f32),
-            pltpu.VMEM((parts, 2 * ROWS, TILES // parts * LANES), f32),
+            pltpu.VMEM((TILES, 2 * ROWS + 8, LANES), f32),
             pltpu.SemaphoreType.DMA((parts,)),
-            pltpu.SemaphoreType.DMA((parts,)),
+            pltpu.SemaphoreType.DMA((TILES,)),
         ],
         compiler_params=pltpu.CompilerParams(vmem_limit_bytes=63 * 1024 * 1024),
         name="lay_out",

time: 74.8 us -> 69.6 us (0.930)
  Pallas kernels: 73.8 us -> 68.5 us
    pallas_call x1, Pallas kernels: 69.4 us -> 64.7 us  [on_device(): pl.pallas_call(functools.partial(main_kernel, count_paired, n_rve, n_mesh...]
where the time goes in v2:
time: 69.6 us; the launch traced here: 69.1 us
  Pallas kernels  68.5 us (98%)
    pallas_call x1, Pallas kernels, on_device(): pl.pallas_call(functools.partial(main_kernel, count_paired, n_rve, n_mesh...  64.7 us
    pallas_call x1, Pallas kernels, lay_out(): pl.pallas_call(lay_out_kernel, in_specs=[hbm, vmem, vmem], out_specs=[hbm...  3.77 us

profile of v2, /device:TPU:96, one launch (start us, length us, event | category | flops | bytes accessed | tf_op | source)
XLA Modules:
  0.0 69.1 jit_solution(697281586522080439)
XLA Ops:
  0.6 64.7 %solve_and_exchange.1 = (f32[3,4]{1,0:T(4,128)}, f32[6,16]{1,0:T(8,128)}, f32[2,32,48,128]{3,2,1,0:T(8,128)}) custom-call(f32[3,4]{1,0:T(4,128)} %disp_h.1, f32[3,8,16]{2,1,0:T(8,128)} %grads_h.1, f32[1,16]{1,0:T(1,128)} %bitcast.12, s32[2,8]{1,0:T(2,128)} %bitcast.11, s32[2,8]{1,0:T(2,128)} %halo_h.1, s32[1,16]{1,0:T(1,128)} %bitcast.13, s32[1,16]{1,0:T(1,128)} %bitcast.14, ...), custom_call_target="tpu_custom_call" | custom-call | tf_op jit(solution)/shard_map/solve_and_exchange/pallas_call | solution.py:737
  65.3 3.8 %lay_out.1 = (f32[96,4096]{1,0:T(8,128)}, f32[3,4]{1,0:T(4,128)}, f32[6,16]{1,0:T(8,128)}) custom-call(f32[2,32,48,128]{3,2,1,0:T(8,128)} %get-tuple-element.9.got_h, f32[3,4]{1,0:T(4,128)} %get-tuple-element.10.nodal_ref, f32[6,16]{1,0:T(8,128)} %get-tuple-element.11.stress_ref), custom_call_target="tpu_custom_call" | custom-call | tf_op jit(solution)/shard_map/lay_out/pallas_call | solution.py:670

commit v3 on v2

--- a/solution.py
+++ b/solution.py
@@ -17,6 +17,11 @@
 HALF = 8
 ROWS = COMPS * HALF
 SPAN = 8 * HALF
+SENT = 4 * HALF
+SHORT = 3 * HALF
+EXTRA = 13
+MIXED_LANE = 112
+ENCODE, CHOOSE, DECODE, TABLE_ROWS = 21, 39, 41, 56
 MESH = pl.DeviceIdType.MESH
 f32 = jnp.float32
 bf16 = jnp.bfloat16
@@ -37,6 +42,7 @@
                 seen.add((y, z))
                 seen.add(((-y) % RES, (-z) % RES))
                 pairs.append((y, z))
+    pairs.sort(key=lambda q: RES // 2 in q)
     lane_a = pairs + [(0, 0), (0, 8)]
     lane_b = pairs + [(8, 0), (8, 8)]
     return np.array(lane_a), np.array(lane_b), len(pairs)
@@ -65,6 +71,35 @@
     return 0.5 * (one(kx, ky, kz) + one(-kx, -ky, -kz))
 
 
+def transport_rows(k):
+    xi = np.array([i if i < RES // 2 else i - RES for i in k], np.float64)
+    size = np.sqrt((xi * xi).sum())
+    n = xi / size if size > 0 else xi
+    edge = [i == RES // 2 for i in k]
+    back = np.zeros((6, 3))
+    mixed = {}
+    for c, (i, j) in enumerate(index_pairs):
+        if i == j:
+            back[c, i] = n[i]
+        elif edge[i] == edge[j]:
+            back[c, i], back[c, j] = 0.5 * n[j], 0.5 * n[i]
+        else:
+            mixed[c] = True
+    rows = np.zeros(TABLE_ROWS)
+    into = np.linalg.pinv(back)
+    rows[ENCODE : ENCODE + 18] = into.reshape(-1)
+    first, second = (sorted(mixed, reverse=True) + [5, 4])[:2]
+    rows[CHOOSE], rows[CHOOSE + 1] = float(first == 5), float(second == 4)
+    rows[DECODE : DECODE + 3] = n
+    rows[DECODE + 3 : DECODE + 9] = back[3, 1], back[3, 2], back[4, 0], back[4, 2], back[5, 0], back[5, 1]
+    if mixed:
+        rows[DECODE + 9] = float(first == 5)
+        rows[DECODE + 10] = float(first == 4)
+        rows[DECODE + 11] = float(second == 4)
+        rows[DECODE + 12] = float(second == 3)
+    return rows
+
+
 @functools.lru_cache(None)
 def tables():
     lane_a, lane_b, count = half_planes()
@@ -79,7 +114,8 @@
     forward = np.concatenate(
         [np.cos(phase(lane_a)), np.where(paired, -np.sin(phase(lane_b)), np.cos(phase(lane_b)))], axis=1
     )
-    coef = np.zeros((RES, 2, 24, LANES))
+    coef = np.zeros((RES, 2, TABLE_ROWS, LANES))
+    moved_by = functools.lru_cache(None)(transport_rows)
     for slot in range(RES):
         for part in range(2):
             ky, kz, kx, scale = [], [], [], []
@@ -93,6 +129,8 @@
                     y, z = lane_a[lane] if slot < RES // 2 else lane_b[lane]
                     x, weight = (slot if slot < RES // 2 else RES - slot), 0.5
                 ky.append(y), kz.append(z), kx.append(x), scale.append(weight / RES**3)
+            for lane in range(LANES):
+                coef[slot, part, :, lane] = moved_by((kx[lane] % RES, int(ky[lane]) % RES, int(kz[lane]) % RES))
             matrix = green_matrix(np.array(kx), np.array(ky), np.array(kz)) * np.array(scale)
             for row, (c, d) in enumerate(coef_rows):
                 coef[slot, part, row] = matrix[c, d]
@@ -188,19 +226,19 @@
 def main_kernel(
     count_paired, n_rve, n_mesh,
     disp_h, grads_h, weight_h, conn_h, halo_h, owner_h, sweeps_h, warm_h, moduli_h, plane_h, coef_h,
-    nodal_o, stress_o, got2,
-    warm_v, moduli_v, plane_v, coef_v, field, mod, tau_h, tau_l, spec, got1_a, got1_b, stage,
+    nodal_o, stress_o, out_h,
+    warm_v, moduli_v, plane_v, coef_v, field, mod, tau_h, tau_l, spec_a, spec_b, payload, got1_a, got1_b, got2, mixed, sums_v, stage,
     tile_v, gathered, halo_out, halo_in, force_out, force_in, own_out, own_in,
     perm_v, perm_s, table_v, table_s, column_v,
     disp_s, grads_v, weight_v, conn_v, halo_v, owner_v, sweeps_v, small_sem,
-    in_sem, idx_sem, gather_send, gather_recv, halo_send, halo_recv,
+    in_sem, out_sem, idx_sem, gather_send, gather_recv, halo_send, halo_recv,
     send1, recv1, send2, recv2, fhalo_send, fhalo_recv, own_send, own_recv,
 ):
     me = lax.axis_index("rve")
     part = lax.axis_index("mesh")
     others = n_rve - 1
     got1 = (got1_a, got1_b)
-    last_row = others * SPAN + HALF - 1
+    last_row = others * SENT + HALF - 1
     has_below = part > 0
     has_above = part < n_mesh - 1
 
@@ -376,7 +414,7 @@
     sends_b = sends.astype(bf16)
     order = jnp.dot(lower, sends_b, preferred_element_type=f32)
     places = jnp.dot(sends_b, upper, preferred_element_type=f32)
-    rows_at = iota((n_rve, LANES), 0).astype(f32) * float(SPAN) + places
+    rows_at = iota((n_rve, LANES), 0).astype(f32) * float(SENT) + places
     table = jnp.zeros((HALF, LANES), f32)
     for k in range(HALF):
         row = sum_rows(jnp.where((sends > 0.5) & (order == float(k)), rows_at, 0.0))
@@ -420,7 +458,10 @@
     big_loads[2].wait()
     odd_lane = iota((HALF, LANES), 1) >= count_paired
 
-    def sweep(half, number):
+    def table_row(k, part_at, row):
+        return coef_v[k, part_at, row : row + 1, :]
+
+    def spectrum_of(half, number, spec):
         def polarize(u, carry):
             for b in range(2):
                 cats = [[] for _ in range(COMPS)]
@@ -465,18 +506,22 @@
         lax.fori_loop(0, COMPS, forward, 0, unroll=2)
 
         def green(k, carry):
+            again = column_v[half, 2, 0] > float(number) + 0.5
             for part_at in range(2):
                 ins = [spec[k, part_at, c] for c in range(COMPS)]
-                rows = [coef_v[k, part_at, r : r + 1, :] for r in range(len(coef_rows))]
+                rows = [table_row(k, part_at, r) for r in range(len(coef_rows))]
                 for c in range(COMPS):
                     total = rows[coef_at[(c, 0)]] * ins[0]
                     for d in range(1, COMPS):
                         total = total + rows[coef_at[(c, d)]] * ins[d]
+                    if number > 0:
+                        total = jnp.where(again, total, spec_a[k, part_at, c])
                     spec[k, part_at, c] = total
             return carry
 
         lax.fori_loop(0, RES, green, 0, unroll=2)
 
+    def strain_from(half, spec, take):
         def backward(c, carry):
             z = [(spec[k, 0, c], spec[k, 1, c]) for k in range(RES)]
             for k in range(1, 8):
@@ -494,84 +539,203 @@
             high, low = split_bf16(lined)
             fluct = three_pass(high, low, plane_v[2], plane_v[3])
             level = column_v[half, 1, c]
-            again = column_v[half, 2, 0] > float(number) + 0.5
+            take(
+                c,
+                [
+                    level - fluct[t // 2 * HALF : (t // 2 + 1) * HALF, t % 2 * LANES : (t % 2 + 1) * LANES]
+                    for t in range(TILES)
+                ],
+            )
+            return carry
+
+        lax.fori_loop(0, COMPS, backward, 0, unroll=2)
+
+    def keep_field(half):
+        def take(c, tiles):
             at = pl.multiple_of(c * HALF, HALF)
-            for x in range(RES):
-                for b in range(2):
-                    new = level - fluct[x * HALF : (x + 1) * HALF, b * LANES : (b + 1) * LANES]
-                    t = 2 * x + b
-                    if number > 0:
-                        new = jnp.where(again, new, field[half, t, pl.ds(at, HALF), :])
-                    field[half, t, pl.ds(at, HALF), :] = new
-            return carry
-
-        lax.fori_loop(0, COMPS, backward, 0, unroll=2)
+            for t in range(TILES):
+                field[half, t, pl.ds(at, HALF), :] = tiles[t]
+
+        strain_from(half, spec_a, take)
 
     def mean_stress(half):
-        def body(t, sums):
-            eps = [field[half, t, c * HALF : (c + 1) * HALF, :] for c in range(COMPS)]
-            lam = mod[half, t, 0:HALF, :]
-            shear = mod[half, t, HALF : 2 * HALF, :]
-            new = [sums[c] + shear * eps[c] for c in range(COMPS)]
-            return (*new, sums[6] + lam * (eps[0] + eps[1] + eps[2]))
-
-        sums = lax.fori_loop(0, TILES, body, tuple(jnp.zeros((HALF, LANES), f32) for _ in range(7)), unroll=4)
+        def take(c, tiles):
+            for which in range(2):
+                parts = [
+                    mod[half, t, which * HALF : (which + 1) * HALF, :] * tiles[t] for t in range(TILES)
+                ]
+                while len(parts) > 1:
+                    parts = [p + q for p, q in zip(parts[::2], parts[1::2])]
+                sums_v[which, c] = parts[0]
+
+        strain_from(half, spec_b, take)
+        pressure = sums_v[0, 0] + sums_v[0, 1] + sums_v[0, 2]
         result = []
         for c in range(COMPS):
-            total = 2.0 * sums[c]
+            total = 2.0 * sums_v[1, c]
             if c < 3:
-                total = total + sums[6]
+                total = total + pressure
             result.append(sum_lanes(total) * (1.0 / 4096.0))
         return result
 
+    packed_group = iota((HALF, LANES), 1) // 16
+
+    def encode(half):
+        def extras(k, part_at, eps):
+            first = jnp.where(table_row(k, part_at, CHOOSE) > 0.5, eps[5], eps[4])
+            second = jnp.where(table_row(k, part_at, CHOOSE + 1) > 0.5, eps[4], eps[3])
+            return first, second
+
+        def body(i, carry):
+            packed = jnp.zeros((HALF, LANES), f32)
+            for step in range(2):
+                k = 2 * i + step
+                for part_at in range(2):
+                    eps = [spec_b[k, part_at, c] for c in range(COMPS)]
+                    for j in range(3):
+                        total = table_row(k, part_at, ENCODE + 6 * j) * eps[0]
+                        for c in range(1, COMPS):
+                            total = total + table_row(k, part_at, ENCODE + 6 * j + c) * eps[c]
+                        payload[half, 2 * k + part_at, j * HALF : (j + 1) * HALF, :] = total
+                    for e, value in enumerate(extras(k, part_at, eps)):
+                        piece = (2 * step + part_at) * 2 + e
+                        shift = (16 * piece + 16) % LANES
+                        if shift:
+                            value = pltpu.roll(value, shift, 1)
+                        packed = jnp.where(packed_group == piece, value, packed)
+            payload[half, i, SHORT:SENT, :] = packed
+            return carry
+
+        lax.fori_loop(0, 8, body, 0)
+        for part_at in range(2):
+            eps = [spec_b[RES // 2, part_at, c] for c in range(COMPS)]
+            for e, value in enumerate(extras(RES // 2, part_at, eps)):
+                payload[half, 8 + 2 * part_at + e, SHORT:SENT, :] = value
+        levels = jnp.zeros((HALF, LANES), f32)
+        for c in range(COMPS):
+            levels = jnp.where(lane8 == float(c), column_v[half, 1, c], levels)
+        payload[half, EXTRA - 1, SHORT:SENT, :] = levels
+
+    def decode(half):
+        def restore(k, part_at, first, second):
+            d = [got2[half, 2 * k + part_at, j * HALF : (j + 1) * HALF, :] for j in range(3)]
+            row = [table_row(k, part_at, DECODE + r) for r in range(13)]
+            for c in range(3):
+                spec_a[k, part_at, c] = row[c] * d[c]
+            spec_a[k, part_at, 3] = row[3] * d[1] + row[4] * d[2] + row[12] * second
+            spec_a[k, part_at, 4] = row[5] * d[0] + row[6] * d[2] + (row[10] * first + row[11] * second)
+            spec_a[k, part_at, 5] = row[7] * d[0] + row[8] * d[1] + row[9] * first
+
+        def body(i, carry):
+            packed = got2[half, i, SHORT:SENT, :]
+            for step in range(2):
+                for part_at in range(2):
+                    values = []
+                    for e in range(2):
+                        piece = (2 * step + part_at) * 2 + e
+                        shift = (LANES - (16 * piece + 16) % LANES) % LANES
+                        values.append(pltpu.roll(packed, shift, 1) if shift else packed)
+                    restore(2 * i + step, part_at, *values)
+            return carry
+
+        lax.fori_loop(0, 8, body, 0)
+        for part_at in range(2):
+            restore(
+                RES // 2, part_at,
+                got2[half, 8 + 2 * part_at, SHORT:SENT, :], got2[half, 9 + 2 * part_at, SHORT:SENT, :],
+            )
+        levels = got2[half, EXTRA - 1, SHORT:SENT, :]
+        for c in range(COMPS):
+            column_v[half, 1, c] = jnp.broadcast_to(levels[:, c : c + 1], (HALF, LANES))
+
+        def take(c, tiles):
+            at = pl.multiple_of(c * 2 * HALF, 2 * HALF)
+            for t in range(TILES):
+                mixed[t, pl.ds(at + half, HALF, stride=2), :] = tiles[t]
+
+        strain_from(half, spec_a, take)
+
+    long_rows = jnp.where(me < EXTRA, 1, 0) == 1
+
+    def by_me(action):
+        @pl.when(long_rows)
+        def _():
+            action(SENT)
+
+        @pl.when(jnp.logical_not(long_rows))
+        def _():
+            action(SHORT)
+
+    def wait_mine(sem):
+        by_me(lambda rows: wait_bytes(got2.at[0, pl.ds(0, others), pl.ds(0, rows), :], sem))
+
+    def wait_all(sem):
+        full = EXTRA * SENT + (n_rve - EXTRA) * SHORT
+        by_me(lambda rows: wait_bytes(got1_a.at[pl.ds(0, full - rows), :], sem))
+
     def send_spread(half):
-        rows = pl.multiple_of(me * SPAN, SPAN)
-        got1[half][pl.ds(rows, ROWS), :] = field[half, me, pl.ds(0, ROWS), :]
+        at = pl.multiple_of(me * SENT, SENT)
+        for j in range(4):
+            rows = pl.multiple_of(me * SENT + j * HALF, HALF)
+            got1[half][pl.ds(rows, HALF), :] = payload[half, me, j * HALF : (j + 1) * HALF, :]
 
         def body(k, carry):
             to = lax.rem(me + k, n_rve)
-            pltpu.make_async_remote_copy(
-                field.at[half, to, pl.ds(0, ROWS), :], got1[half].at[pl.ds(rows, ROWS), :], send1.at[half], recv1.at[half],
-                device_id={"rve": to}, device_id_type=MESH,
-            ).start()
+
+            def send(rows):
+                pltpu.make_async_remote_copy(
+                    payload.at[half, to, pl.ds(0, rows), :], got1[half].at[pl.ds(at, rows), :],
+                    send1.at[half], recv1.at[half], device_id={"rve": to}, device_id_type=MESH,
+                ).start()
+
+            @pl.when(to < EXTRA)
+            def _():
+                send(SENT)
+
+            @pl.when(to >= EXTRA)
+            def _():
+                send(SHORT)
+
             return carry
 
         lax.fori_loop(1, n_rve, body, 0)
 
     def send_owned(half):
-        wait_bytes(got2.at[half, pl.ds(0, others)], recv1.at[half])
+        wait_mine(recv1.at[half])
+
+        def collect(to):
+            for at in range(HALF):
+                row = jnp.clip(table_s[at, to], 0, last_row)
+                stage[half, to, pl.ds(at, 4, stride=HALF), :] = got1[half][pl.ds(row, 4, stride=HALF), :]
 
         def body(k, carry):
             to = lax.rem(me + k, n_rve)
-            for at in range(HALF):
-                row = jnp.clip(table_s[at, to], 0, last_row)
-                stage[half, to, pl.ds(at, COMPS, stride=HALF), :] = got1[half][
-                    pl.ds(row, COMPS, stride=HALF), :
-                ]
-
-            @pl.when(k > 0)
-            def _():
-                pltpu.make_async_remote_copy(
-                    stage.at[half, to, pl.ds(0, ROWS), :], got2.at[half, me], send2.at[half], recv2.at[half],
-                    device_id={"rve": to}, device_id_type=MESH,
+            collect(to)
+            by_me(
+                lambda rows: pltpu.make_async_remote_copy(
+                    stage.at[half, to, pl.ds(0, rows), :], got2.at[half, me, pl.ds(0, rows), :],
+                    send2.at[half], recv2.at[half], device_id={"rve": to}, device_id_type=MESH,
                 ).start()
-
+            )
             return carry
 
         lax.fori_loop(1, n_rve, body, 0)
-        body(0, 0)
-        keep = pltpu.make_async_copy(stage.at[half, me, pl.ds(0, ROWS), :], got2.at[half, me], in_sem.at[4 + half])
-        keep.start()
-        return keep
+        collect(me)
+        for j in range(4):
+            got2[half, me, j * HALF : (j + 1) * HALF, :] = stage[half, me, j * HALF : (j + 1) * HALF, :]
 
     load_table.wait()
-    sweep(0, 0)
-    sweep(0, 1)
+    spectrum_of(0, 0, spec_a)
+    keep_field(0)
+    spectrum_of(0, 1, spec_b)
+    encode(0)
     send_spread(0)
     stress = [mean_stress(0)]
-    sweep(1, 0)
-    keep0 = send_owned(0)
-    sweep(1, 1)
+    spectrum_of(1, 0, spec_a)
+    keep_field(1)
+    send_owned(0)
+    spectrum_of(1, 1, spec_b)
+    encode(1)
     send_spread(1)
     stress.append(mean_stress(1))
 
@@ -607,7 +771,9 @@
     own_out[...] = own_tile
     own_in[me] = own_tile
     to_all(own_out, own_in.at[me], own_send, own_recv)
-    keep1 = send_owned(1)
+    send_owned(1)
+    wait_all(recv2.at[0])
+    decode(0)
     wait_bytes(own_in.at[pl.ds(0, others)], own_recv)
     total = jnp.sum(own_in[...], axis=0)
     mine = jnp.zeros((4, LANES), f32)
@@ -615,15 +781,26 @@
         mine = jnp.where(lane4 == node, sum_lanes(jnp.where(lane4 == 4 * me + node, total, 0.0)), mine)
     nodal_o[...] = mine[:3, :4]
 
-    keep0.wait()
-    keep1.wait()
-    for half in range(2):
-        wait_bytes(got2.at[half, pl.ds(0, others)], recv2.at[half])
+    wait_all(recv2.at[1])
+    decode(1)
+
+    def copy_out(t):
+        at = pl.multiple_of(t * LANES, LANES)
+        return pltpu.make_async_copy(
+            mixed.at[t, pl.ds(0, 2 * ROWS), :], out_h.at[:, pl.ds(at, LANES)], out_sem
+        )
+
+    def start_out(t, carry):
+        copy_out(t).start()
+        return carry
+
+    lax.fori_loop(0, TILES, start_out, 0)
+    wait_bytes(mixed.at[:, pl.ds(0, 2 * ROWS), :], out_sem)
     wait_bytes(gathered.at[pl.ds(0, others)], gather_send)
     wait_bytes(own_in.at[pl.ds(0, others)], own_send)
     for half in range(2):
-        wait_bytes(got2.at[half, pl.ds(0, others)], send1.at[half])
-        wait_bytes(got2.at[half, pl.ds(0, others)], send2.at[half])
+        wait_all(send1.at[half])
+        wait_mine(send2.at[half])
     for send, source in ((halo_send, halo_out), (fhalo_send, force_out)):
         @pl.when(has_below)
         def _(send=send, source=source):
@@ -634,57 +811,43 @@
             wait_bytes(source, send.at[1])
 
 
-def lay_out_kernel(got_h, nodal_ref, stress_ref, out_h, nodal_o, stress_o, taken, mixed, in_sem, out_sem):
-    parts = taken.shape[0]
-    group = TILES // parts
-
-    def copy_in(at):
-        return pltpu.make_async_copy(got_h.at[:, pl.ds(at * group, group)], taken.at[at], in_sem.at[at])
-
-    def copy_out(t):
-        return pltpu.make_async_copy(
-            mixed.at[t, pl.ds(0, 2 * ROWS), :], out_h.at[:, pl.ds(t * LANES, LANES)], out_sem.at[t]
-        )
-
-    for at in range(parts):
-        copy_in(at).start()
+def hand_over_kernel(field_h, nodal_ref, stress_ref, field_o, nodal_o, stress_o, held, in_sem, out_sem):
+    starts = range(0, 2 * ROWS, HALF)
+    taken = [
+        pltpu.make_async_copy(field_h.at[pl.ds(at, HALF), :], held.at[pl.ds(at, HALF), :], in_sem.at[n])
+        for n, at in enumerate(starts)
+    ]
+    given = [
+        pltpu.make_async_copy(held.at[pl.ds(at, HALF), :], field_o.at[pl.ds(at, HALF), :], out_sem.at[n])
+        for n, at in enumerate(starts)
+    ]
+    for copy in taken:
+        copy.start()
     nodal_o[...] = nodal_ref[...]
     stress_o[...] = stress_ref[...]
-    for at in range(parts):
-        copy_in(at).wait()
-        for t in range(group):
-            for c in range(COMPS):
-                for half in range(2):
-                    mixed[at * group + t, pl.ds(2 * HALF * c + half, HALF, stride=2), :] = taken[
-                        at, half, t, c * HALF : (c + 1) * HALF, :
-                    ]
-            copy_out(at * group + t).start()
-    for t in range(TILES):
-        copy_out(t).wait()
-
-
-def lay_out(got, nodal, stress):
-    parts = 8
+    for copy, onward in zip(taken, given):
+        copy.wait()
+        onward.start()
+    for onward in given:
+        onward.wait()
+
+
+def hand_over(field, nodal, stress):
     vmem = pl.BlockSpec(memory_space=pltpu.VMEM)
     hbm = pl.BlockSpec(memory_space=pltpu.HBM)
     return pl.pallas_call(
-        lay_out_kernel,
+        hand_over_kernel,
         in_specs=[hbm, vmem, vmem],
         out_specs=[hbm, vmem, vmem],
-        out_shape=[
-            jax.ShapeDtypeStruct((2 * ROWS, TILES * LANES), f32),
-            jax.ShapeDtypeStruct(nodal.shape, f32),
-            jax.ShapeDtypeStruct(stress.shape, f32),
-        ],
+        out_shape=[jax.ShapeDtypeStruct(x.shape, f32) for x in (field, nodal, stress)],
         scratch_shapes=[
-            pltpu.VMEM((parts, 2, TILES // parts, ROWS, LANES), f32),
-            pltpu.VMEM((TILES, 2 * ROWS + 8, LANES), f32),
-            pltpu.SemaphoreType.DMA((parts,)),
-            pltpu.SemaphoreType.DMA((TILES,)),
+            pltpu.VMEM(field.shape, f32),
+            pltpu.SemaphoreType.DMA((2 * ROWS // HALF,)),
+            pltpu.SemaphoreType.DMA((2 * ROWS // HALF,)),
         ],
         compiler_params=pltpu.CompilerParams(vmem_limit_bytes=63 * 1024 * 1024),
-        name="lay_out",
-    )(got, nodal, stress)
+        name="hand_over",
+    )(field, nodal, stress)
 
 
 def solution(mesh):
@@ -707,8 +870,13 @@
             pltpu.VMEM((COMPS, RES * HALF, PLANE), bf16),
             pltpu.VMEM((COMPS, RES * HALF, PLANE), bf16),
             pltpu.VMEM((RES, 2, COMPS, HALF, LANES), f32),
-            pltpu.VMEM((n_rve * SPAN, LANES), f32),
-            pltpu.VMEM((n_rve * SPAN, LANES), f32),
+            pltpu.VMEM((RES, 2, COMPS, HALF, LANES), f32),
+            pltpu.VMEM((2, n_rve, SENT, LANES), f32),
+            pltpu.VMEM((n_rve * SENT + SPAN, LANES), f32),
+            pltpu.VMEM((n_rve * SENT + SPAN, LANES), f32),
+            pltpu.VMEM((2, n_rve, SENT, LANES), f32),
+            pltpu.VMEM((TILES, 2 * ROWS + HALF, LANES), f32),
+            pltpu.VMEM((2, COMPS, HALF, LANES), f32),
             pltpu.VMEM((2, n_rve, SPAN, LANES), f32),
             pltpu.VMEM((4, LANES), f32),
             pltpu.VMEM((n_rve, 4, LANES), f32),
@@ -731,17 +899,17 @@
             pltpu.VMEM((1, points), jnp.int32),
             pltpu.VMEM((1, points), jnp.int32),
             dma((7,)),
-            dma((6,)), dma((2,)), dma, dma, dma((2,)), dma((2,)),
+            dma((4,)), dma, dma((2,)), dma, dma, dma((2,)), dma((2,)),
             dma((2,)), dma((2,)), dma((2,)), dma((2,)), dma((2,)), dma((2,)), dma, dma,
         ]
-        nodal, stress, got = pl.pallas_call(
+        nodal, stress, out = pl.pallas_call(
             functools.partial(main_kernel, count_paired, n_rve, n_mesh),
             in_specs=[hbm] * 11,
             out_specs=[vmem, vmem, hbm],
             out_shape=[
                 jax.ShapeDtypeStruct((3, 4), f32),
                 jax.ShapeDtypeStruct((COMPS, points), f32),
-                jax.ShapeDtypeStruct((2, n_rve, ROWS, LANES), f32),
+                jax.ShapeDtypeStruct((2 * ROWS, voxels), f32),
             ],
             scratch_shapes=scratch,
             compiler_params=pltpu.CompilerParams(
@@ -753,7 +921,7 @@
             owner.reshape(1, points), sweeps.reshape(1, points), warm, moduli,
             jnp.asarray(planes), jnp.asarray(coef),
         )
-        micro, nodal, stress = lay_out(got, nodal, stress)
+        micro, nodal, stress = hand_over(out, nodal, stress)
         micro = micro.reshape(COMPS, points, voxels).transpose(1, 0, 2)
         return nodal, stress, micro
 

time: 69.6 us -> 58.1 us (0.83)
  Pallas kernels: 68.5 us -> 57 us
    pallas_call x1, Pallas kernels: 64.7 us -> 53.4 us  [on_device(): pl.pallas_call(functools.partial(main_kernel, count_paired, n_rve, n_mesh...]
where the time goes in v3:
time: 58.1 us; the launch traced here: 57.6 us
  Pallas kernels  57 us (98%)
  between operations  0.64 us (1%)
    pallas_call x1, Pallas kernels, on_device(): pl.pallas_call(functools.partial(main_kernel, count_paired, n_rve, n_mesh...  53.4 us
    pallas_call x1, Pallas kernels, hand_over(): pl.pallas_call(hand_over_kernel, in_specs=[hbm, vmem, vmem], out_specs=[h...  3.6 us

profile of v3, /device:TPU:96, one launch (start us, length us, event | category | flops | bytes accessed | tf_op | source)
XLA Modules:
  0.0 57.6 jit_solution(10043701518378529109)
XLA Ops:
  0.6 53.4 %solve_and_exchange.1 = (f32[3,4]{1,0:T(4,128)}, f32[6,16]{1,0:T(8,128)}, f32[96,4096]{1,0:T(8,128)}) custom-call(f32[3,4]{1,0:T(4,128)} %disp_h.1, f32[3,8,16]{2,1,0:T(8,128)} %grads_h.1, f32[1,16]{1,0:T(1,128)} %bitcast.12, s32[2,8]{1,0:T(2,128)} %bitcast.11, s32[2,8]{1,0:T(2,128)} %halo_h.1, s32[1,16]{1,0:T(1,128)} %bitcast.13, s32[1,16]{1,0:T(1,128)} %bitcast.14, ...), custom_call_target="tpu_custom_call" | custom-call | tf_op jit(solution)/shard_map/solve_and_exchange/pallas_call | solution.py:905
  54.0 3.6 %hand_over.1 = (f32[96,4096]{1,0:T(8,128)}, f32[3,4]{1,0:T(4,128)}, f32[6,16]{1,0:T(8,128)}) custom-call(f32[96,4096]{1,0:T(8,128)} %get-tuple-element.9.field_h, f32[3,4]{1,0:T(4,128)} %get-tuple-element.10.nodal_ref, f32[6,16]{1,0:T(8,128)} %get-tuple-element.11.stress_ref), custom_call_target="tpu_custom_call" | custom-call | tf_op jit(solution)/shard_map/hand_over/pallas_call | solution.py:838

commit v4 on v3

--- a/solution.py
+++ b/solution.py
@@ -227,7 +227,7 @@
     count_paired, n_rve, n_mesh,
     disp_h, grads_h, weight_h, conn_h, halo_h, owner_h, sweeps_h, warm_h, moduli_h, plane_h, coef_h,
     nodal_o, stress_o, out_h,
-    warm_v, moduli_v, plane_v, coef_v, field, mod, tau_h, tau_l, spec_a, spec_b, payload, got1_a, got1_b, got2, mixed, sums_v, stage,
+    warm_v, moduli_v, plane_v, coef_v, field, mod, tau_h, tau_l, spec_0, spec_a, spec_b, payload, got1_a, got1_b, got2, mixed, sums_v, stage,
     tile_v, gathered, halo_out, halo_in, force_out, force_in, own_out, own_in,
     perm_v, perm_s, table_v, table_s, column_v,
     disp_s, grads_v, weight_v, conn_v, halo_v, owner_v, sweeps_v, small_sem,
@@ -237,6 +237,10 @@
     me = lax.axis_index("rve")
     part = lax.axis_index("mesh")
     others = n_rve - 1
+
+    def after_me(k):
+        return jnp.where(me + k >= n_rve, me + k - n_rve, me + k)
+
     got1 = (got1_a, got1_b)
     last_row = others * SENT + HALF - 1
     has_below = part > 0
@@ -273,11 +277,8 @@
 
     barrier = pltpu.get_barrier_semaphore()
 
-    def greet(k, carry):
-        pl.semaphore_signal(barrier, inc=1, device_id={"rve": lax.rem(me + k, n_rve)}, device_id_type=MESH)
-        return carry
-
-    lax.fori_loop(1, n_rve, greet, 0)
+    for k in range(1, n_rve):
+        pl.semaphore_signal(barrier, inc=1, device_id={"rve": after_me(k)}, device_id_type=MESH)
 
     @pl.when(has_below)
     def _():
@@ -318,13 +319,14 @@
 
     def to_all(source, target, send, recv):
         def body(k, carry):
-            to = lax.rem(me + k, n_rve)
+            to = after_me(k)
             pltpu.make_async_remote_copy(
                 source, target, send, recv, device_id={"rve": to}, device_id_type=MESH
             ).start()
             return carry
 
-        lax.fori_loop(1, n_rve, body, 0)
+        for k in range(1, n_rve):
+            body(k, 0)
 
     def wait_bytes(view, sem):
         pltpu.make_async_copy(view, view, sem).wait()
@@ -359,6 +361,111 @@
         0, TILES, add_up, tuple(jnp.zeros((HALF, LANES), f32) for _ in range(2 * COMPS)), unroll=4
     )
     means = [[sum_lanes(sums[half * COMPS + c]) * (1.0 / 4096.0) for c in range(COMPS)] for half in range(2)]
+
+    big_loads[1].wait()
+    big_loads[2].wait()
+    odd_lane = iota((HALF, LANES), 1) >= count_paired
+
+    def table_row(k, part_at, row):
+        return coef_v[k, part_at, row : row + 1, :]
+
+    def forward_into(planes, put):
+        def forward(c, carry):
+            planed = three_pass(tau_h[c], tau_l[c], plane_v[0], plane_v[1])
+            values = [
+                (planed[x * HALF : (x + 1) * HALF, :LANES], planed[x * HALF : (x + 1) * HALF, LANES:])
+                for x in range(RES)
+            ]
+            z = sixteen_point(values, -1)
+            for k in range(1, 8):
+                a, b = z[k], z[RES - k]
+                z[k] = (jnp.where(odd_lane, a[0] + b[0], a[0]), jnp.where(odd_lane, a[1] - b[1], a[1]))
+                z[RES - k] = (jnp.where(odd_lane, a[1] + b[1], b[0]), jnp.where(odd_lane, b[0] - a[0], b[1]))
+            for k in range(RES):
+                put(k, 0, c, z[k][0])
+                put(k, 1, c, z[k][1])
+            return carry
+
+        lax.fori_loop(0, planes, forward, 0, unroll=2)
+
+    def polarize_into(half, first):
+        def polarize(u, carry):
+            for b in range(2):
+                cats = [[] for _ in range(8)]
+                for step in range(2):
+                    t = (2 * u + step) * 2 + b
+                    eps = [field[half, t, c * HALF : (c + 1) * HALF, :] for c in range(COMPS)]
+                    if first:
+                        eps = [eps[c] - means[half][c] for c in range(COMPS)]
+                    lam = mod[half, t, 0:HALF, :] - 1.1
+                    shear = 2.0 * mod[half, t, HALF : 2 * HALF, :] - 2.2
+                    pressure = lam * (eps[0] + eps[1] + eps[2])
+                    double = shear + shear
+                    for c in range(3):
+                        cats[c].append(shear * eps[c] + pressure)
+                    for c in range(3, 6):
+                        cats[c].append(double * eps[c])
+                    if first:
+                        cats[6].append(lam)
+                        cats[7].append(shear)
+                for c in range(8 if first else COMPS):
+                    high, low = split_bf16(jnp.concatenate(cats[c], axis=0))
+                    at = pl.multiple_of(u * 16, 16)
+                    tau_h[c, pl.ds(at, 16), b * LANES : (b + 1) * LANES] = high
+                    tau_l[c, pl.ds(at, 16), b * LANES : (b + 1) * LANES] = low
+            return carry
+
+        lax.fori_loop(0, 8, polarize, 0, unroll=2)
+
+    def start_spectrum(half):
+        def put(k, part_at, c, value):
+            spec_0[half, k, part_at, c] = value
+
+        polarize_into(half, True)
+        forward_into(8, put)
+
+    def apply_green(half, k, part_at, ins, spec, keep):
+        rows = [table_row(k, part_at, r) for r in range(len(coef_rows))]
+        for c in range(COMPS):
+            total = rows[coef_at[(c, 0)]] * ins[0]
+            for d in range(1, COMPS):
+                total = total + rows[coef_at[(c, d)]] * ins[d]
+            if keep is not None:
+                total = jnp.where(keep, total, spec_a[k, part_at, c])
+            spec[k, part_at, c] = total
+
+    def first_spectrum(half):
+        def green(k, carry):
+            level = [column_v[half, 1, c] for c in range(COMPS)]
+            level = level[:3] + [2.0 * x for x in level[3:]]
+            whole = level[0] + level[1] + level[2]
+            for part_at in range(2):
+                ins = [spec_0[half, k, part_at, c] for c in range(8)]
+                pressure = whole * ins[6]
+                ins = [ins[c] + level[c] * ins[7] for c in range(COMPS)]
+                ins = [ins[c] + pressure if c < 3 else ins[c] for c in range(COMPS)]
+                apply_green(half, k, part_at, ins, spec_a, None)
+            return carry
+
+        lax.fori_loop(0, RES, green, 0, unroll=2)
+
+    def second_spectrum(half):
+        def put(k, part_at, c, value):
+            spec_b[half, k, part_at, c] = value
+
+        polarize_into(half, False)
+        forward_into(COMPS, put)
+
+        def green(k, carry):
+            again = column_v[half, 2, 0] > 1.5
+            for part_at in range(2):
+                ins = [spec_b[half, k, part_at, c] for c in range(COMPS)]
+                apply_green(half, k, part_at, ins, spec_b.at[half], again)
+            return carry
+
+        lax.fori_loop(0, RES, green, 0, unroll=2)
+
+    start_spectrum(0)
 
     wait_bytes(gathered.at[pl.ds(0, others)], gather_recv)
     moved = jnp.sum(gathered[...], axis=0)
@@ -431,6 +538,7 @@
         far_hot.append(jnp.where(col - float(LANES) == lane8, 1.0, 0.0))
     first_element = iota((HALF, 16), 1) < 8
 
+    start_spectrum(1)
     take_halo(halo_out, halo_in, halo_recv)
     below, above = halo_in[0], halo_in[1]
     spread_disp = []
@@ -449,77 +557,9 @@
     for c in range(COMPS):
         for half in range(2):
             col = macro_cols[c][half * HALF : (half + 1) * HALF]
-            column_v[half, 0, c] = jnp.broadcast_to(col - means[half][c], (HALF, LANES))
             column_v[half, 1, c] = jnp.broadcast_to(col, (HALF, LANES))
     for half in range(2):
         column_v[half, 2, 0] = jnp.broadcast_to(count_col[half * HALF : (half + 1) * HALF], (HALF, LANES))
-
-    big_loads[1].wait()
-    big_loads[2].wait()
-    odd_lane = iota((HALF, LANES), 1) >= count_paired
-
-    def table_row(k, part_at, row):
-        return coef_v[k, part_at, row : row + 1, :]
-
-    def spectrum_of(half, number, spec):
-        def polarize(u, carry):
-            for b in range(2):
-                cats = [[] for _ in range(COMPS)]
-                for step in range(2):
-                    t = (2 * u + step) * 2 + b
-                    eps = [field[half, t, c * HALF : (c + 1) * HALF, :] for c in range(COMPS)]
-                    if number == 0:
-                        eps = [eps[c] + column_v[half, 0, c] for c in range(COMPS)]
-                    lam = mod[half, t, 0:HALF, :] - 1.1
-                    shear = 2.0 * mod[half, t, HALF : 2 * HALF, :] - 2.2
-                    pressure = lam * (eps[0] + eps[1] + eps[2])
-                    double = shear + shear
-                    for c in range(3):
-                        cats[c].append(shear * eps[c] + pressure)
-                    for c in range(3, 6):
-                        cats[c].append(double * eps[c])
-                for c in range(COMPS):
-                    high, low = split_bf16(jnp.concatenate(cats[c], axis=0))
-                    at = pl.multiple_of(u * 16, 16)
-                    tau_h[c, pl.ds(at, 16), b * LANES : (b + 1) * LANES] = high
-                    tau_l[c, pl.ds(at, 16), b * LANES : (b + 1) * LANES] = low
-            return carry
-
-        lax.fori_loop(0, 8, polarize, 0, unroll=2)
-
-        def forward(c, carry):
-            planed = three_pass(tau_h[c], tau_l[c], plane_v[0], plane_v[1])
-            values = [
-                (planed[x * HALF : (x + 1) * HALF, :LANES], planed[x * HALF : (x + 1) * HALF, LANES:])
-                for x in range(RES)
-            ]
-            z = sixteen_point(values, -1)
-            for k in range(1, 8):
-                a, b = z[k], z[RES - k]
-                z[k] = (jnp.where(odd_lane, a[0] + b[0], a[0]), jnp.where(odd_lane, a[1] - b[1], a[1]))
-                z[RES - k] = (jnp.where(odd_lane, a[1] + b[1], b[0]), jnp.where(odd_lane, b[0] - a[0], b[1]))
-            for k in range(RES):
-                spec[k, 0, c] = z[k][0]
-                spec[k, 1, c] = z[k][1]
-            return carry
-
-        lax.fori_loop(0, COMPS, forward, 0, unroll=2)
-
-        def green(k, carry):
-            again = column_v[half, 2, 0] > float(number) + 0.5
-            for part_at in range(2):
-                ins = [spec[k, part_at, c] for c in range(COMPS)]
-                rows = [table_row(k, part_at, r) for r in range(len(coef_rows))]
-                for c in range(COMPS):
-                    total = rows[coef_at[(c, 0)]] * ins[0]
-                    for d in range(1, COMPS):
-                        total = total + rows[coef_at[(c, d)]] * ins[d]
-                    if number > 0:
-                        total = jnp.where(again, total, spec_a[k, part_at, c])
-                    spec[k, part_at, c] = total
-            return carry
-
-        lax.fori_loop(0, RES, green, 0, unroll=2)
 
     def strain_from(half, spec, take):
         def backward(c, carry):
@@ -568,7 +608,7 @@
                     parts = [p + q for p, q in zip(parts[::2], parts[1::2])]
                 sums_v[which, c] = parts[0]
 
-        strain_from(half, spec_b, take)
+        strain_from(half, spec_b.at[half], take)
         pressure = sums_v[0, 0] + sums_v[0, 1] + sums_v[0, 2]
         result = []
         for c in range(COMPS):
@@ -591,7 +631,7 @@
             for step in range(2):
                 k = 2 * i + step
                 for part_at in range(2):
-                    eps = [spec_b[k, part_at, c] for c in range(COMPS)]
+                    eps = [spec_b[half, k, part_at, c] for c in range(COMPS)]
                     for j in range(3):
                         total = table_row(k, part_at, ENCODE + 6 * j) * eps[0]
                         for c in range(1, COMPS):
@@ -608,7 +648,7 @@
 
         lax.fori_loop(0, 8, body, 0)
         for part_at in range(2):
-            eps = [spec_b[RES // 2, part_at, c] for c in range(COMPS)]
+            eps = [spec_b[half, RES // 2, part_at, c] for c in range(COMPS)]
             for e, value in enumerate(extras(RES // 2, part_at, eps)):
                 payload[half, 8 + 2 * part_at + e, SHORT:SENT, :] = value
         levels = jnp.zeros((HALF, LANES), f32)
@@ -680,7 +720,7 @@
             got1[half][pl.ds(rows, HALF), :] = payload[half, me, j * HALF : (j + 1) * HALF, :]
 
         def body(k, carry):
-            to = lax.rem(me + k, n_rve)
+            to = after_me(k)
 
             def send(rows):
                 pltpu.make_async_remote_copy(
@@ -698,7 +738,8 @@
 
             return carry
 
-        lax.fori_loop(1, n_rve, body, 0)
+        for k in range(1, n_rve):
+            body(k, 0)
 
     def send_owned(half):
         wait_mine(recv1.at[half])
@@ -709,7 +750,7 @@
                 stage[half, to, pl.ds(at, 4, stride=HALF), :] = got1[half][pl.ds(row, 4, stride=HALF), :]
 
         def body(k, carry):
-            to = lax.rem(me + k, n_rve)
+            to = after_me(k)
             collect(to)
             by_me(
                 lambda rows: pltpu.make_async_remote_copy(
@@ -719,25 +760,22 @@
             )
             return carry
 
-        lax.fori_loop(1, n_rve, body, 0)
+        for k in range(1, n_rve):
+            body(k, 0)
         collect(me)
         for j in range(4):
             got2[half, me, j * HALF : (j + 1) * HALF, :] = stage[half, me, j * HALF : (j + 1) * HALF, :]
 
     load_table.wait()
-    spectrum_of(0, 0, spec_a)
-    keep_field(0)
-    spectrum_of(0, 1, spec_b)
-    encode(0)
-    send_spread(0)
-    stress = [mean_stress(0)]
-    spectrum_of(1, 0, spec_a)
-    keep_field(1)
-    send_owned(0)
-    spectrum_of(1, 1, spec_b)
-    encode(1)
-    send_spread(1)
-    stress.append(mean_stress(1))
+    for half in range(2):
+        first_spectrum(half)
+        keep_field(half)
+        if half == 1:
+            send_owned(0)
+        second_spectrum(half)
+        encode(half)
+        send_spread(half)
+    stress = [mean_stress(0), mean_stress(1)]
 
     weights = weight_v[...]
     sigma = []
@@ -774,27 +812,26 @@
     send_owned(1)
     wait_all(recv2.at[0])
     decode(0)
+    wait_all(recv2.at[1])
+    decode(1)
+
+    def copy_out(t):
+        at = pl.multiple_of(t * LANES, LANES)
+        return pltpu.make_async_copy(
+            mixed.at[t, pl.ds(0, 2 * ROWS), :], out_h.at[:, pl.ds(at, LANES)], out_sem
+        )
+
+    def start_out(t, carry):
+        copy_out(t).start()
+        return carry
+
+    lax.fori_loop(0, TILES, start_out, 0)
     wait_bytes(own_in.at[pl.ds(0, others)], own_recv)
     total = jnp.sum(own_in[...], axis=0)
     mine = jnp.zeros((4, LANES), f32)
     for node in range(4):
         mine = jnp.where(lane4 == node, sum_lanes(jnp.where(lane4 == 4 * me + node, total, 0.0)), mine)
     nodal_o[...] = mine[:3, :4]
-
-    wait_all(recv2.at[1])
-    decode(1)
-
-    def copy_out(t):
-        at = pl.multiple_of(t * LANES, LANES)
-        return pltpu.make_async_copy(
-            mixed.at[t, pl.ds(0, 2 * ROWS), :], out_h.at[:, pl.ds(at, LANES)], out_sem
-        )
-
-    def start_out(t, carry):
-        copy_out(t).start()
-        return carry
-
-    lax.fori_loop(0, TILES, start_out, 0)
     wait_bytes(mixed.at[:, pl.ds(0, 2 * ROWS), :], out_sem)
     wait_bytes(gathered.at[pl.ds(0, others)], gather_send)
     wait_bytes(own_in.at[pl.ds(0, others)], own_send)
@@ -811,20 +848,16 @@
             wait_bytes(source, send.at[1])
 
 
-def hand_over_kernel(field_h, nodal_ref, stress_ref, field_o, nodal_o, stress_o, held, in_sem, out_sem):
-    starts = range(0, 2 * ROWS, HALF)
-    taken = [
-        pltpu.make_async_copy(field_h.at[pl.ds(at, HALF), :], held.at[pl.ds(at, HALF), :], in_sem.at[n])
-        for n, at in enumerate(starts)
+def hand_over_kernel(field_h, nodal_h, stress_h, field_o, nodal_o, stress_o, held, nodal_v, stress_v, in_sem, out_sem):
+    through = [
+        (field_h.at[pl.ds(at, HALF), :], held.at[pl.ds(at, HALF), :], field_o.at[pl.ds(at, HALF), :])
+        for at in range(0, 2 * ROWS, HALF)
     ]
-    given = [
-        pltpu.make_async_copy(held.at[pl.ds(at, HALF), :], field_o.at[pl.ds(at, HALF), :], out_sem.at[n])
-        for n, at in enumerate(starts)
-    ]
+    through = [(nodal_h, nodal_v, nodal_o), (stress_h, stress_v, stress_o)] + through
+    taken = [pltpu.make_async_copy(a, b, in_sem.at[n]) for n, (a, b, _) in enumerate(through)]
+    given = [pltpu.make_async_copy(b, c, out_sem.at[n]) for n, (_, b, c) in enumerate(through)]
     for copy in taken:
         copy.start()
-    nodal_o[...] = nodal_ref[...]
-    stress_o[...] = stress_ref[...]
     for copy, onward in zip(taken, given):
         copy.wait()
         onward.start()
@@ -833,18 +866,15 @@
 
 
 def hand_over(field, nodal, stress):
-    vmem = pl.BlockSpec(memory_space=pltpu.VMEM)
     hbm = pl.BlockSpec(memory_space=pltpu.HBM)
+    count = 2 * ROWS // HALF + 2
     return pl.pallas_call(
         hand_over_kernel,
-        in_specs=[hbm, vmem, vmem],
-        out_specs=[hbm, vmem, vmem],
+        in_specs=[hbm, hbm, hbm],
+        out_specs=[hbm, hbm, hbm],
         out_shape=[jax.ShapeDtypeStruct(x.shape, f32) for x in (field, nodal, stress)],
-        scratch_shapes=[
-            pltpu.VMEM(field.shape, f32),
-            pltpu.SemaphoreType.DMA((2 * ROWS // HALF,)),
-            pltpu.SemaphoreType.DMA((2 * ROWS // HALF,)),
-        ],
+        scratch_shapes=[pltpu.VMEM(x.shape, f32) for x in (field, nodal, stress)]
+        + [pltpu.SemaphoreType.DMA((count,)), pltpu.SemaphoreType.DMA((count,))],
         compiler_params=pltpu.CompilerParams(vmem_limit_bytes=63 * 1024 * 1024),
         name="hand_over",
     )(field, nodal, stress)
@@ -867,10 +897,11 @@
             pltpu.VMEM(coef.shape, f32),
             pltpu.VMEM((2, TILES, SPAN, LANES), f32),
             pltpu.VMEM((2, TILES, SPAN, LANES), f32),
-            pltpu.VMEM((COMPS, RES * HALF, PLANE), bf16),
-            pltpu.VMEM((COMPS, RES * HALF, PLANE), bf16),
+            pltpu.VMEM((8, RES * HALF, PLANE), bf16),
+            pltpu.VMEM((8, RES * HALF, PLANE), bf16),
+            pltpu.VMEM((2, RES, 2, 8, HALF, LANES), f32),
             pltpu.VMEM((RES, 2, COMPS, HALF, LANES), f32),
-            pltpu.VMEM((RES, 2, COMPS, HALF, LANES), f32),
+            pltpu.VMEM((2, RES, 2, COMPS, HALF, LANES), f32),
             pltpu.VMEM((2, n_rve, SENT, LANES), f32),
             pltpu.VMEM((n_rve * SENT + SPAN, LANES), f32),
             pltpu.VMEM((n_rve * SENT + SPAN, LANES), f32),

time: 58.1 us -> 55 us (0.947)
  Pallas kernels: 57 us -> 53.9 us
    pallas_call x1, Pallas kernels: 53.4 us -> 51.6 us  [on_device(): pl.pallas_call(functools.partial(main_kernel, count_paired, n_rve, n_mesh...]
    pallas_call x1, Pallas kernels: 3.6 us -> 2.37 us  [hand_over(): pl.pallas_call(hand_over_kernel, in_specs=[hbm, hbm, hbm], out_specs=[hbm...]
where the time goes in v4:
time: 55 us; the launch traced here: 54.6 us
  Pallas kernels  53.9 us (98%)
  between operations  0.64 us (1%)
    pallas_call x1, Pallas kernels, on_device(): pl.pallas_call(functools.partial(main_kernel, count_paired, n_rve, n_mesh...  51.6 us
    pallas_call x1, Pallas kernels, hand_over(): pl.pallas_call(hand_over_kernel, in_specs=[hbm, hbm, hbm], out_specs=[hbm...  2.37 us

profile of v4, /device:TPU:96, one launch (start us, length us, event | category | flops | bytes accessed | tf_op | source)
XLA Modules:
  0.0 54.6 jit_solution(10740543570361873611)
XLA Ops:
  0.6 51.6 %solve_and_exchange.1 = (f32[3,4]{1,0:T(4,128)}, f32[6,16]{1,0:T(8,128)}, f32[96,4096]{1,0:T(8,128)}) custom-call(f32[3,4]{1,0:T(4,128)} %disp_h.1, f32[3,8,16]{2,1,0:T(8,128)} %grads_h.1, f32[1,16]{1,0:T(1,128)} %bitcast.12, s32[2,8]{1,0:T(2,128)} %bitcast.11, s32[2,8]{1,0:T(2,128)} %halo_h.1, s32[1,16]{1,0:T(1,128)} %bitcast.13, s32[1,16]{1,0:T(1,128)} %bitcast.14, ...), custom_call_target="tpu_custom_call" | custom-call | tf_op jit(solution)/shard_map/solve_and_exchange/pallas_call | solution.py:936
  52.2 2.4 %hand_over.1 = (f32[96,4096]{1,0:T(8,128)}, f32[3,4]{1,0:T(4,128)}, f32[6,16]{1,0:T(8,128)}) custom-call(f32[96,4096]{1,0:T(8,128)} %get-tuple-element.9.field_h, f32[3,4]{1,0:T(4,128)} %get-tuple-element.10.nodal_h, f32[6,16]{1,0:T(8,128)} %get-tuple-element.11.stress_h), custom_call_target="tpu_custom_call" | custom-call | tf_op jit(solution)/shard_map/hand_over/pallas_call | solution.py:871

commit v5 on v4

--- a/solution.py
+++ b/solution.py
@@ -386,7 +386,7 @@
                 put(k, 1, c, z[k][1])
             return carry
 
-        lax.fori_loop(0, planes, forward, 0, unroll=2)
+        lax.fori_loop(0, planes, forward, 0, unroll=planes // 2)
 
     def polarize_into(half, first):
         def polarize(u, carry):
@@ -588,7 +588,7 @@
             )
             return carry
 
-        lax.fori_loop(0, COMPS, backward, 0, unroll=2)
+        lax.fori_loop(0, COMPS, backward, 0, unroll=3)
 
     def keep_field(half):
         def take(c, tiles):
@@ -646,7 +646,7 @@
             payload[half, i, SHORT:SENT, :] = packed
             return carry
 
-        lax.fori_loop(0, 8, body, 0)
+        lax.fori_loop(0, 8, body, 0, unroll=2)
         for part_at in range(2):
             eps = [spec_b[half, RES // 2, part_at, c] for c in range(COMPS)]
             for e, value in enumerate(extras(RES // 2, part_at, eps)):
@@ -678,7 +678,7 @@
                     restore(2 * i + step, part_at, *values)
             return carry
 
-        lax.fori_loop(0, 8, body, 0)
+        lax.fori_loop(0, 8, body, 0, unroll=2)
         for part_at in range(2):
             restore(
                 RES // 2, part_at,

time: 55 us -> 53.8 us (0.978)
  Pallas kernels: 53.9 us -> 52.7 us
    pallas_call x1, Pallas kernels: 51.6 us -> 50.3 us  [on_device(): pl.pallas_call(functools.partial(main_kernel, count_paired, n_rve, n_mesh...]
where the time goes in v5:
time: 53.8 us; the launch traced here: 53.3 us
  Pallas kernels  52.7 us (98%)
  between operations  0.64 us (1%)
    pallas_call x1, Pallas kernels, on_device(): pl.pallas_call(functools.partial(main_kernel, count_paired, n_rve, n_mesh...  50.3 us
    pallas_call x1, Pallas kernels, hand_over(): pl.pallas_call(hand_over_kernel, in_specs=[hbm, hbm, hbm], out_specs=[hbm...  2.37 us

profile of v5, /device:TPU:96, one launch (start us, length us, event | category | flops | bytes accessed | tf_op | source)
XLA Modules:
  0.0 53.3 jit_solution(1622337509705005945)
XLA Ops:
  0.6 50.3 %solve_and_exchange.1 = (f32[3,4]{1,0:T(4,128)}, f32[6,16]{1,0:T(8,128)}, f32[96,4096]{1,0:T(8,128)}) custom-call(f32[3,4]{1,0:T(4,128)} %disp_h.1, f32[3,8,16]{2,1,0:T(8,128)} %grads_h.1, f32[1,16]{1,0:T(1,128)} %bitcast.12, s32[2,8]{1,0:T(2,128)} %bitcast.11, s32[2,8]{1,0:T(2,128)} %halo_h.1, s32[1,16]{1,0:T(1,128)} %bitcast.13, s32[1,16]{1,0:T(1,128)} %bitcast.14, ...), custom_call_target="tpu_custom_call" | custom-call | tf_op jit(solution)/shard_map/solve_and_exchange/pallas_call | solution.py:936
  51.0 2.4 %hand_over.1 = (f32[96,4096]{1,0:T(8,128)}, f32[3,4]{1,0:T(4,128)}, f32[6,16]{1,0:T(8,128)}) custom-call(f32[96,4096]{1,0:T(8,128)} %get-tuple-element.9.field_h, f32[3,4]{1,0:T(4,128)} %get-tuple-element.10.nodal_h, f32[6,16]{1,0:T(8,128)} %get-tuple-element.11.stress_h), custom_call_target="tpu_custom_call" | custom-call | tf_op jit(solution)/shard_map/hand_over/pallas_call | solution.py:871
